TPU v7x, 512 devices: a whole 4x8x8 slice. The times are simulated.
512 devices in a mesh: seq: 64 (over z, y), mp: 8 (over x, core).
Axes of the slice: x: 4, y: 8, z: 8, core: 2. Of those that a mesh axis runs over, the one named last changes fastest.
Arguments:
- query: bfloat16 [16384, 3072], P('seq', 'mp'), may hold values from -4.5 to 4.5
- key: bfloat16 [16384, 3072], P('seq', 'mp'), may hold values from -4.5 to 4.5
- value: bfloat16 [16384, 3072], P('seq', 'mp'), may hold values from -6 to 6
- clip_lengths: int32 [4, 4], replicated, may hold values from 0 to 4096, as said below
Outputs:
- attended: bfloat16 [16384, 3072], P(('seq', 'mp'))
Inputs may be any that keep to these rules, and one draw needn't show every extreme that they name: `clip_lengths`: each row sums to 4096; a clip slot may be empty; in some bucket one clip fills all 4096 tokens.
All inputs are finite; a program needn't handle non-finite values.
Results may differ from a plain program's by a relative error of at most 0.01.
Values may be sent and summed in bfloat16 or wider, within the bound.
No kernel may reach another device: no remote copies, remote signals or barrier semaphores. Data moves between devices by JAX's collectives and lax.ppermute only.
A program may use at most 64 MiB of HBM per device.

v0:
```python
import jax
import jax.numpy as jnp
from jax import lax
from jax.sharding import PartitionSpec as P

HD = 128


NEG = -1e30


def from_partner(array, axis, apart):
    return lax.ppermute(array, axis, [(i, i ^ 1 << apart) for i in range(lax.axis_size(axis))])


def shards(query, key, value, clip_lengths):
    tok_rows = query.shape[0]
    width = query.shape[1]
    heads = width // HD
    scale = 1.0 / HD**0.5
    group = lax.axis_size("seq") // 4
    levels = group.bit_length() - 1
    span = tok_rows * group
    buckets = clip_lengths.shape[0]
    slots = clip_lengths.shape[1]
    me_index = lax.axis_index("seq")
    start = me_index * tok_rows
    home_bucket = me_index // group
    ends = jnp.cumsum(clip_lengths, axis=1)
    bucket_ids = jnp.arange(buckets, dtype=jnp.int32)

    def clip_of(places):
        bucket = places // span
        offset = places - bucket * span
        hits = jnp.sum((offset[:, None, None] >= ends[None, :, :]).astype(jnp.int32), axis=2)
        pick = bucket[:, None] == bucket_ids[None, :]
        inner = jnp.sum(jnp.where(pick, hits, 0), axis=1)
        return bucket * slots + inner

    limit = home_bucket * span + span
    q_ids = clip_of(start + jnp.arange(tok_rows, dtype=jnp.int32))
    queries = query.reshape(tok_rows, heads, HD)

    def attend(carry, q_rows, q_clip, key_block, value_block, first, bound):
        count = key_block.shape[0]
        keys = key_block.reshape(count, heads, HD)
        values = value_block.reshape(count, heads, HD)
        k_ids = clip_of(first + jnp.arange(count, dtype=jnp.int32))

        def update(state):
            top_old, total_old, summed_old = state
            score = (
                jnp.einsum("qhd,khd->hqk", q_rows, keys, preferred_element_type=jnp.float32) * scale
            )
            keep = (q_clip[:, None] == k_ids[None, :])[None]
            score = jnp.where(keep, score, NEG)
            top_new = jnp.maximum(top_old, jnp.max(score, axis=-1))
            weight = jnp.where(keep, jnp.exp(score - top_new[:, :, None]), 0.0)
            factor = jnp.exp(top_old - top_new)
            total_new = total_old * factor + jnp.sum(weight, axis=-1)
            added = jnp.einsum(
                "hqk,khd->qhd",
                weight.astype(jnp.bfloat16),
                values,
                preferred_element_type=jnp.float32,
            )
            summed_new = summed_old * jnp.transpose(factor)[:, :, None] + added
            return (top_new, total_new, summed_new)

        needed = first < bound
        return lax.cond(needed, update, lambda state: state, carry)

    initial = (
        jnp.full((heads, tok_rows), NEG, jnp.float32),
        jnp.zeros((heads, tok_rows), jnp.float32),
        jnp.zeros((tok_rows, heads, HD), jnp.float32),
    )
    held = (key, value)
    pieces = [(held, start)]
    for bit in range(levels):
        received = from_partner((held[0], held[1]), "seq", bit)
        stride = 2**bit
        own_base = me_index // stride * stride
        partner_upper = me_index // stride % 2
        pieces.append((received, (own_base + stride - 2 * stride * partner_upper) * tok_rows))
        if bit + 1 < levels:
            upper = me_index // 2**bit % 2 == 1
            lower_keys = jnp.where(upper, received[0], held[0])
            higher_keys = jnp.where(upper, held[0], received[0])
            lower_values = jnp.where(upper, received[1], held[1])
            higher_values = jnp.where(upper, held[1], received[1])
            held = (
                jnp.concatenate([lower_keys, higher_keys], axis=0),
                jnp.concatenate([lower_values, higher_values], axis=0),
            )
    carry = initial
    for piece, first in pieces:
        sweep_carry = carry
        keys_all, values_all = piece
        sweep_count = keys_all.shape[0]
        size = 512
        whole = sweep_count // size * size
        if whole > 0:
            key_blocks = keys_all.reshape(whole // size, size, width)
            value_blocks = values_all.reshape(whole // size, size, width)
            firsts = first + jnp.arange(whole // size, dtype=jnp.int32) * size

            def step(state, items):
                return (attend(state, queries, q_ids, items[0], items[1], items[2], limit), None)

            sweep_carry, unused = lax.scan(step, sweep_carry, (key_blocks, value_blocks, firsts))
        if sweep_count > whole:
            sweep_carry = attend(
                sweep_carry, queries, q_ids, keys_all, values_all, first + whole, limit
            )
        carry = sweep_carry
    top_all, total_all, summed_all = carry
    result = (
        (summed_all / jnp.transpose(total_all)[:, :, None])
        .reshape(tok_rows, width)
        .astype(jnp.bfloat16)
    )
    return lax.all_to_all(result, "mp", split_axis=0, concat_axis=1, tiled=True)


def solution(mesh):
    in_specs = (P("seq", "mp"), P("seq", "mp"), P("seq", "mp"), P())
    out_specs = P(("seq", "mp"), None)
    return jax.shard_map(shards, mesh=mesh, in_specs=in_specs, out_specs=out_specs, check_vma=False)
```

profile of v0, /device:TPU:1, one launch (start us, length us, event | category | flops | bytes accessed | tf_op | source)
XLA Modules:
  0.0 258.1 jit_solution(3211704166920266424)
XLA Ops:
  0.0 1.1 copy.126
  1.1 4.0 %collective-permute-start.1 = (bf16[256,384]{0,1:T(8,128)(2,1)S(1)}, bf16[256,384]{0,1:T(8,128)(2,1)S(1)}, u32[]{:S(2)}, u32[]{:S(2)}) collective-permute-start(bf16[256,384]{0,1:T(8,128)(2,1)S(1)} %copy.126), channel_id=1, source_target_pairs={{0,8},{8,0},{16,24},{24,16},{32,40},{40,32},{48,56},{56,48},{64,72... | collective-permute-start | bytes 589832 | tf_op jit(solution)/shard_map/ppermute | solution.py:13
  5.1 1.1 copy.125
  6.2 1.9 collective-permute-start
  8.1 0.9 reduce_window_sum.11
  10.9 1.7 collective-permute-done
  12.7 5.1 %collective-permute-start.3 = (bf16[512,384]{0,1:T(8,128)(2,1)S(1)}, bf16[512,384]{0,1:T(8,128)(2,1)S(1)}, u32[]{:S(2)}, u32[]{:S(2)}) collective-permute-start(bf16[512,384]{0,1:T(8,128)(2,1)S(1)} %pad_maximum_fusion.5), channel_id=1, source_target_pairs={{0,16},{8,24},{16,0},{24,8},{32,48},{40,56},{48,32},{56,40},{64,80... | collective-permute-start | bytes 1179656 | tf_op jit(solution)/shard_map/ppermute | solution.py:13
  18.5 1.9 collective-permute-start.2
  20.4 22.3 %collective-permute-done.3 = bf16[512,384]{0,1:T(8,128)(2,1)S(1)} collective-permute-done((bf16[512,384]{0,1:T(8,128)(2,1)S(1)}, bf16[512,384]{0,1:T(8,128)(2,1)S(1)}, u32[]{:S(2)}, u32[]{:S(2)}) %collective-permute-start.3) | collective-permute-done | bytes 393248 | tf_op jit(solution)/shard_map/ppermute | solution.py:13
  42.9 1.0 pad_maximum_fusion.3
  43.9 9.2 %collective-permute-start.5 = (bf16[1024,384]{0,1:T(8,128)(2,1)}, bf16[1024,384]{0,1:T(8,128)(2,1)S(1)}, u32[]{:S(2)}, u32[]{:S(2)}) collective-permute-start(bf16[1024,384]{0,1:T(8,128)(2,1)} %pad_maximum_fusion.3), channel_id=1, source_target_pairs={{0,32},{8,40},{16,48},{24,56},{32,0},{40,8},{48,16},{56,24},{64,96... | collective-permute-start | bytes 2359304 | tf_op jit(solution)/shard_map/ppermute | solution.py:13
  53.8 1.0 pad_maximum_fusion.2
  54.7 74.3 %collective-permute-start.4 = (bf16[1024,384]{0,1:T(8,128)(2,1)}, bf16[1024,384]{0,1:T(8,128)(2,1)}, u32[]{:S(2)}, u32[]{:S(2)}) collective-permute-start(bf16[1024,384]{0,1:T(8,128)(2,1)} %pad_maximum_fusion.2), channel_id=1, source_target_pairs={{0,32},{8,40},{16,48},{24,56},{32,0},{40,8},{48,16},{56,24},{64,96... | collective-permute-start | bytes 2359304 | tf_op jit(solution)/shard_map/ppermute | solution.py:13
  129.9 3.7 %conditional.5 = (f32[3,256]{1,0:T(4,128)}, f32[3,256]{1,0:T(4,128)S(1)}, f32[256,3,128]{2,0,1:T(8,128)S(1)}) conditional(s32[]{:T(128)} %convert_element_type.75, () %tuple.129, (s32[256]{0:T(256)S(1)}, bf16[256,3,128]{0,2,1:T(8,128)(2,1)S(1)}, bf16[256,3,128]{0,2,1:T(8,128)(2,1)S(1)}, bf16[256,3,128]{0,2,1:T(8,128)(2,1)S(1)}) %tuple.268), branch_computations={%region_3.4_spmd, %region_4.7_spmd} | conditional | flops 102599680 | bytes 3639320 | solution.py:71
  130.9 0.8 fusion.7
  131.8 1.1 fusion.5
  134.6 1.3 pad_maximum_fusion.1
  135.8 4.0 %collective-permute-start.7 = (bf16[2048,384]{0,1:T(8,128)(2,1)}, bf16[2048,384]{0,1:T(8,128)(2,1)}, u32[]{:S(2)}, u32[]{:S(2)}) collective-permute-start(bf16[2048,384]{0,1:T(8,128)(2,1)} %pad_maximum_fusion.1), channel_id=1, source_target_pairs={{0,64},{8,72},{16,80},{24,88},{32,96},{40,104},{48,112},{56,120},{... | collective-permute-start | bytes 4718600 | tf_op jit(solution)/shard_map/ppermute | solution.py:13
  139.8 24.1 %collective-permute-done.4 = bf16[1024,384]{0,1:T(8,128)(2,1)} collective-permute-done((bf16[1024,384]{0,1:T(8,128)(2,1)}, bf16[1024,384]{0,1:T(8,128)(2,1)}, u32[]{:S(2)}, u32[]{:S(2)}) %collective-permute-start.4) | collective-permute-done | bytes 786464 | tf_op jit(solution)/shard_map/ppermute | solution.py:13
  163.9 1.4 broadcast_select_fusion.3
  165.4 1.3 pad_maximum_fusion
  166.6 4.0 %collective-permute-start.6 = (bf16[2048,384]{0,1:T(8,128)(2,1)}, bf16[2048,384]{0,1:T(8,128)(2,1)}, u32[]{:S(2)}, u32[]{:S(2)}) collective-permute-start(bf16[2048,384]{0,1:T(8,128)(2,1)} %pad_maximum_fusion), channel_id=1, source_target_pairs={{0,64},{8,72},{16,80},{24,88},{32,96},{40,104},{48,112},{56,120},{... | collective-permute-start | bytes 4718600 | tf_op jit(solution)/shard_map/ppermute | solution.py:13
  170.8 3.1 %conditional.6 = ((f32[3,256]{1,0:T(4,128)}, f32[3,256]{1,0:T(4,128)S(1)}, f32[256,3,128]{2,0,1:T(8,128)S(1)})) conditional(s32[]{:T(128)} %convert_element_type.74, (f32[3,256]{1,0:T(4,128)}, f32[3,256]{1,0:T(4,128)S(1)}, f32[256,3,128]{2,0,1:T(8,128)S(1)}) %conditional.5, (s32[256]{0:T(256)S(1)}, s32[256]{0:T(256)S(1)}, ...), branch_computations={%region_9.10_spmd, %region_10.13_spmd} | conditional | flops 102697216 | bytes 4048928 | solution.py:71
  173.9 3.9 %conditional.7 = ((f32[3,256]{1,0:T(4,128)}, f32[3,256]{1,0:T(4,128)S(1)}, f32[256,3,128]{2,0,1:T(8,128)S(1)})) conditional(s32[]{:T(128)} %convert_element_type.73, (f32[3,256]{1,0:T(4,128)}, f32[3,256]{1,0:T(4,128)S(1)}, f32[256,3,128]{2,0,1:T(8,128)S(1)}) %get-tuple-element.1937, (s32[256]{0:T(256)S(1)}, s32[512]{0:T(512)S(1)}, ...), branch_computations={%region_13.14_spmd, %region_14.19_spmd.clone} | conditional | flops 205220608 | bytes 7142956 | solution.py:71
  176.6 0.7 multiply_add_fusion.3
  177.9 1.2 copy.177
  179.1 14.8 %while.40 = (s32[]{:T(128)}, f32[3,256]{1,0:T(4,128)}, f32[3,256]{1,0:T(4,128)S(1)}, f32[256,3,128]{2,0,1:T(8,128)S(1)}, s32[2]{0:T(128)S(1)}, /*index=5*/s32[]{...) while((s32[]{:T(128)}, f32[3,256]{1,0:T(4,128)}, ...), condition=%wide.region_26.27_spmd.clone, body=%wide.region_19.26_spmd.clone.sunk | while | flops 205249792 | bytes 8755687 | solution.py:111
  182.2 4.4 %conditional.12 = ((f32[3,256]{1,0:T(4,128)}, f32[3,256]{1,0:T(4,128)S(1)}, f32[256,3,128]{2,0,1:T(8,128)S(1)})) conditional(s32[]{:T(128)} %convert_element_type.109, (f32[3,256]{1,0:T(4,128)}, f32[3,256]{1,0:T(4,128)S(1)}, f32[256,3,128]{2,0,1:T(8,128)S(1)}) %tuple.228, (s32[256]{0:T(256)S(1)}, s32[512]{0:T(512)S(1)}, s32[512]{0:T(512)S(1)}, ...), branch_computations={%region_20.20_spmd, %region_21.25_spmd.clone} | conditional | flops 205220608 | bytes 8707648 | solution.py:71
  185.2 0.7 multiply_add_fusion.1
  189.5 4.4 %conditional.12 = ((f32[3,256]{1,0:T(4,128)}, f32[3,256]{1,0:T(4,128)S(1)}, f32[256,3,128]{2,0,1:T(8,128)S(1)})) conditional(s32[]{:T(128)} %convert_element_type.109, (f32[3,256]{1,0:T(4,128)}, f32[3,256]{1,0:T(4,128)S(1)}, f32[256,3,128]{2,0,1:T(8,128)S(1)}) %tuple.228, (s32[256]{0:T(256)S(1)}, s32[512]{0:T(512)S(1)}, s32[512]{0:T(512)S(1)}, ...), branch_computations={%region_20.20_spmd, %region_21.25_spmd.clone} | conditional | flops 205220608 | bytes 8707648 | solution.py:71
  192.6 0.7 multiply_add_fusion.1
  193.9 1.5 copy.174
  195.5 12.3 %collective-permute-done.6 = bf16[2048,384]{0,1:T(8,128)(2,1)} collective-permute-done((bf16[2048,384]{0,1:T(8,128)(2,1)}, bf16[2048,384]{0,1:T(8,128)(2,1)}, u32[]{:S(2)}, u32[]{:S(2)}) %collective-permute-start.6) | collective-permute-done | bytes 1572896 | tf_op jit(solution)/shard_map/ppermute | solution.py:13
  207.8 2.7 %copy.175 = bf16[48,4,8,512]{3,2,0,1:T(8,128)(2,1)} copy(bf16[48,4,8,512]{3,2,1,0:T(8,128)(2,1)} %bitcast.34) | data formatting | bytes 3145728 | tf_op jit(solution)/shard_map/reshape | solution.py:104
  210.5 35.0 %while.41 = (s32[]{:T(128)}, f32[3,256]{1,0:T(4,128)}, f32[3,256]{1,0:T(4,128)S(1)}, f32[256,3,128]{2,0,1:T(8,128)S(1)}, s32[4]{0:T(128)S(1)}, /*index=5*/s32[]{...) while((s32[]{:T(128)}, f32[3,256]{1,0:T(4,128)}, ...), condition=%wide.region_34.35_spmd.clone, body=%wide.region_27.34_spmd.clone.sunk | while | flops 205249792 | bytes 8755687 | solution.py:111
  213.8 5.5 %conditional.13 = ((f32[3,256]{1,0:T(4,128)}, f32[3,256]{1,0:T(4,128)S(1)}, f32[256,3,128]{2,0,1:T(8,128)S(1)})) conditional(s32[]{:T(128)} %convert_element_type.111, (f32[3,256]{1,0:T(4,128)}, f32[3,256]{1,0:T(4,128)S(1)}, f32[256,3,128]{2,0,1:T(8,128)S(1)}) %tuple.233, (s32[256]{0:T(256)S(1)}, s32[512]{0:T(512)S(1)}, s32[512]{0:T(512)S(1)}, ...), branch_computations={%region_28.28_spmd, %region_29.33_spmd.clone} | conditional | flops 205220608 | bytes 8707648 | solution.py:71
  214.7 1.1 constant_dynamic-slice_fusion.2
  218.0 0.7 multiply_add_fusion.2
  222.6 5.5 %conditional.13 = ((f32[3,256]{1,0:T(4,128)}, f32[3,256]{1,0:T(4,128)S(1)}, f32[256,3,128]{2,0,1:T(8,128)S(1)})) conditional(s32[]{:T(128)} %convert_element_type.111, (f32[3,256]{1,0:T(4,128)}, f32[3,256]{1,0:T(4,128)S(1)}, f32[256,3,128]{2,0,1:T(8,128)S(1)}) %tuple.233, (s32[256]{0:T(256)S(1)}, s32[512]{0:T(512)S(1)}, s32[512]{0:T(512)S(1)}, ...), branch_computations={%region_28.28_spmd, %region_29.33_spmd.clone} | conditional | flops 205220608 | bytes 8707648 | solution.py:71
  223.5 1.1 constant_dynamic-slice_fusion.2
  226.7 0.7 multiply_add_fusion.2
  231.3 5.5 %conditional.13 = ((f32[3,256]{1,0:T(4,128)}, f32[3,256]{1,0:T(4,128)S(1)}, f32[256,3,128]{2,0,1:T(8,128)S(1)})) conditional(s32[]{:T(128)} %convert_element_type.111, (f32[3,256]{1,0:T(4,128)}, f32[3,256]{1,0:T(4,128)S(1)}, f32[256,3,128]{2,0,1:T(8,128)S(1)}) %tuple.233, (s32[256]{0:T(256)S(1)}, s32[512]{0:T(512)S(1)}, s32[512]{0:T(512)S(1)}, ...), branch_computations={%region_28.28_spmd, %region_29.33_spmd.clone} | conditional | flops 205220608 | bytes 8707648 | solution.py:71
  232.3 1.1 constant_dynamic-slice_fusion.2
  235.5 0.7 multiply_add_fusion.2
  240.1 5.5 %conditional.13 = ((f32[3,256]{1,0:T(4,128)}, f32[3,256]{1,0:T(4,128)S(1)}, f32[256,3,128]{2,0,1:T(8,128)S(1)})) conditional(s32[]{:T(128)} %convert_element_type.111, (f32[3,256]{1,0:T(4,128)}, f32[3,256]{1,0:T(4,128)S(1)}, f32[256,3,128]{2,0,1:T(8,128)S(1)}) %tuple.233, (s32[256]{0:T(256)S(1)}, s32[512]{0:T(512)S(1)}, s32[512]{0:T(512)S(1)}, ...), branch_computations={%region_28.28_spmd, %region_29.33_spmd.clone} | conditional | flops 205220608 | bytes 8707648 | solution.py:71
  241.0 1.1 constant_dynamic-slice_fusion.2
  244.3 0.7 multiply_add_fusion.2
  246.1 11.3 %all_to_all.16 = bf16[8,32,384]{2,1,0:T(8,128)(2,1)S(1)} all-to-all(bf16[8,32,384]{2,1,0:T(8,128)(2,1)S(1)} %convert_element_type.80), channel_id=1, replica_groups=mesh['seq'=64,'mp'=8] {'mp'}, dimensions={0} | all-to-all | bytes 393216 | tf_op jit(solution)/shard_map/all_to_all | solution.py:123
  (199 shorter events, 51.7 us)
Async XLA Ops:
  1.1 9.8 %collective-permute-start.1 = (bf16[256,384]{0,1:T(8,128)(2,1)S(1)}, bf16[256,384]{0,1:T(8,128)(2,1)S(1)}, u32[]{:S(2)}, u32[]{:S(2)}) collective-permute-start(bf16[256,384]{0,1:T(8,128)(2,1)S(1)} %copy.126), channel_id=1, source_target_pairs={{0,8},{8,0},{16,24},{24,16},{32,40},{40,32},{48,56},{56,48},{64,72... | collective-permute-start | bytes 589832 | tf_op jit(solution)/shard_map/ppermute | solution.py:13
  6.2 6.4 %collective-permute-start = (bf16[256,384]{0,1:T(8,128)(2,1)S(1)}, bf16[256,384]{0,1:T(8,128)(2,1)S(1)}, u32[]{:S(2)}, u32[]{:S(2)}) collective-permute-start(bf16[256,384]{0,1:T(8,128)(2,1)S(1)} %copy.125), channel_id=1, source_target_pairs={{0,8},{8,0},{16,24},{24,16},{32,40},{40,32},{48,56},{56,48},{64,72... | collective-permute-start | bytes 589832 | tf_op jit(solution)/shard_map/ppermute | solution.py:13
  10.9 7.6 %copy-start.4 = (bf16[256,384]{0,1:T(8,128)(2,1)}, bf16[256,384]{0,1:T(8,128)(2,1)S(1)}, u32[]{:S(2)}) copy-start(bf16[256,384]{0,1:T(8,128)(2,1)S(1)} %collective-permute-done.1) | copy-start | bytes 589828
  12.6 5.9 %copy-start.6 = (bf16[256,384]{0,1:T(8,128)(2,1)}, bf16[256,384]{0,1:T(8,128)(2,1)S(1)}, u32[]{:S(2)}) copy-start(bf16[256,384]{0,1:T(8,128)(2,1)S(1)} %collective-permute-done) | copy-start | bytes 589828
  12.7 30.1 %collective-permute-start.3 = (bf16[512,384]{0,1:T(8,128)(2,1)S(1)}, bf16[512,384]{0,1:T(8,128)(2,1)S(1)}, u32[]{:S(2)}, u32[]{:S(2)}) collective-permute-start(bf16[512,384]{0,1:T(8,128)(2,1)S(1)} %pad_maximum_fusion.5), channel_id=1, source_target_pairs={{0,16},{8,24},{16,0},{24,8},{32,48},{40,56},{48,32},{56,40},{64,80... | collective-permute-start | bytes 1179656 | tf_op jit(solution)/shard_map/ppermute | solution.py:13
  18.5 35.1 %collective-permute-start.2 = (bf16[512,384]{0,1:T(8,128)(2,1)S(1)}, bf16[512,384]{0,1:T(8,128)(2,1)S(1)}, u32[]{:S(2)}, u32[]{:S(2)}) collective-permute-start(bf16[512,384]{0,1:T(8,128)(2,1)S(1)} %pad_maximum_fusion.4), channel_id=1, source_target_pairs={{0,16},{8,24},{16,0},{24,8},{32,48},{40,56},{48,32},{56,40},{64,80... | collective-permute-start | bytes 1179656 | tf_op jit(solution)/shard_map/ppermute | solution.py:13
  42.8 1.1 copy-start.2
  43.9 90.3 %collective-permute-start.5 = (bf16[1024,384]{0,1:T(8,128)(2,1)}, bf16[1024,384]{0,1:T(8,128)(2,1)S(1)}, u32[]{:S(2)}, u32[]{:S(2)}) collective-permute-start(bf16[1024,384]{0,1:T(8,128)(2,1)} %pad_maximum_fusion.3), channel_id=1, source_target_pairs={{0,32},{8,40},{16,48},{24,56},{32,0},{40,8},{48,16},{56,24},{64,96... | collective-permute-start | bytes 2359304 | tf_op jit(solution)/shard_map/ppermute | solution.py:13
  53.6 75.9 %copy-start.8 = (bf16[256,384]{1,0:T(8,128)(2,1)S(1)}, bf16[256,384]{1,0:T(8,128)(2,1)}, u32[]{:S(2)}) copy-start(bf16[256,384]{1,0:T(8,128)(2,1)} %param.18) | copy-start | bytes 589828
  53.6 1.1 copy-start
  54.7 109.2 %collective-permute-start.4 = (bf16[1024,384]{0,1:T(8,128)(2,1)}, bf16[1024,384]{0,1:T(8,128)(2,1)}, u32[]{:S(2)}, u32[]{:S(2)}) collective-permute-start(bf16[1024,384]{0,1:T(8,128)(2,1)} %pad_maximum_fusion.2), channel_id=1, source_target_pairs={{0,32},{8,40},{16,48},{24,56},{32,0},{40,8},{48,16},{56,24},{64,96... | collective-permute-start | bytes 2359304 | tf_op jit(solution)/shard_map/ppermute | solution.py:13
  129.9 4.3 %copy-start.13 = (s32[256]{0:T(256)S(1)}, s32[256]{0:T(256)}, u32[]{:S(2)}) copy-start(s32[256]{0:T(256)} %get-tuple-element.1661) | copy-start | bytes 3076
  135.8 58.1 %collective-permute-start.7 = (bf16[2048,384]{0,1:T(8,128)(2,1)}, bf16[2048,384]{0,1:T(8,128)(2,1)}, u32[]{:S(2)}, u32[]{:S(2)}) collective-permute-start(bf16[2048,384]{0,1:T(8,128)(2,1)} %pad_maximum_fusion.1), channel_id=1, source_target_pairs={{0,64},{8,72},{16,80},{24,88},{32,96},{40,104},{48,112},{56,120},{... | collective-permute-start | bytes 4718600 | tf_op jit(solution)/shard_map/ppermute | solution.py:13
  165.3 5.3 %copy-start.10 = (s32[512]{0:T(512)S(1)}, s32[512]{0:T(512)}, u32[]{:S(2)}) copy-start(s32[512]{0:T(512)} %fusion.78) | copy-start | bytes 6148
  165.3 5.4 %copy-start.5 = (bf16[256,384]{0,1:T(8,128)(2,1)S(1)}, bf16[256,384]{0,1:T(8,128)(2,1)}, u32[]{:S(2)}) copy-start(bf16[256,384]{0,1:T(8,128)(2,1)} %copy-done.4) | copy-start | bytes 589828
  165.3 5.4 %copy-start.7 = (bf16[256,384]{0,1:T(8,128)(2,1)S(1)}, bf16[256,384]{0,1:T(8,128)(2,1)}, u32[]{:S(2)}) copy-start(bf16[256,384]{0,1:T(8,128)(2,1)} %copy-done.6) | copy-start | bytes 589828
  166.6 41.2 %collective-permute-start.6 = (bf16[2048,384]{0,1:T(8,128)(2,1)}, bf16[2048,384]{0,1:T(8,128)(2,1)}, u32[]{:S(2)}, u32[]{:S(2)}) collective-permute-start(bf16[2048,384]{0,1:T(8,128)(2,1)} %pad_maximum_fusion), channel_id=1, source_target_pairs={{0,64},{8,72},{16,80},{24,88},{32,96},{40,104},{48,112},{56,120},{... | collective-permute-start | bytes 4718600 | tf_op jit(solution)/shard_map/ppermute | solution.py:13
  170.7 3.2 %copy-start.1 = (bf16[512,384]{0,1:T(8,128)(2,1)S(1)}, bf16[512,384]{0,1:T(8,128)(2,1)}, u32[]{:S(2)}) copy-start(bf16[512,384]{0,1:T(8,128)(2,1)} %copy-done) | copy-start | bytes 1179652
  170.7 3.2 %copy-start.3 = (bf16[512,384]{0,1:T(8,128)(2,1)S(1)}, bf16[512,384]{0,1:T(8,128)(2,1)}, u32[]{:S(2)}) copy-start(bf16[512,384]{0,1:T(8,128)(2,1)} %copy-done.2) | copy-start | bytes 1179652
  170.7 3.2 %copy-start.9 = (s32[512]{0:T(512)S(1)}, s32[512]{0:T(512)}, u32[]{:S(2)}) copy-start(s32[512]{0:T(512)} %iota_add_fusion.2) | copy-start | bytes 6148
  170.7 3.2 %copy-start.11 = (s32[512]{0:T(512)S(1)}, s32[512]{0:T(512)}, u32[]{:S(2)}) copy-start(s32[512]{0:T(512)} %get-tuple-element.1659) | copy-start | bytes 6148
  170.8 3.2 %copy-start.12 = (s32[512]{0:T(512)S(1)}, s32[512]{0:T(512)}, u32[]{:S(2)}) copy-start(s32[512]{0:T(512)} %get-tuple-element.1660) | copy-start | bytes 6148
  170.8 3.2 %copy-start.14 = (pred[512]{0:T(512)(128)(4,1)S(1)}, pred[512]{0:T(512)(128)(4,1)}, u32[]{:S(2)}) copy-start(pred[512]{0:T(512)(128)(4,1)} %fusion.80) | copy-start | bytes 1540
  177.9 1.3 copy-start.16
  207.8 2.7 %copy-start.15 = (s32[4]{0:T(128)S(1)}, s32[4]{0:T(128)}, u32[]{:S(2)}) copy-start(s32[4]{0:T(128)} %multiply_add_fusion.6) | copy-start | bytes 52
where the time goes:
time: 260 us; the launch traced here: 258 us
  starting transfers between devices  104 us (40%)
  waiting for transfers between devices  60.5 us (23%)
  other arithmetic  45.1 us (17%)
  local copies, waits for them, and re-layouts  22 us (8%)
  blocking collectives  11.3 us (4%)
  matrix products  10.1 us (4%)
  loops' own time  4.25 us (2%)
    ppermute x8, starting transfers between devices, from_partner(): lax.ppermute(array, axis, [(i, i ^ 1 << apart) for i in range(lax.axis_si...  104 us
    ppermute x8, waiting for transfers between devices, from_partner(): lax.ppermute(array, axis, [(i, i ^ 1 << apart) for i in range(lax.axis_si...  60.5 us
    all_to_all x1, blocking collectives, shards(): return lax.all_to_all(result, 'mp', split_axis=0, concat_axis=1, tiled=True)  11.3 us
    dynamic_slice x12, local copies, waits for them, and re-layouts, shards(): lax.scan(step, sweep_carry, (key_blocks, value_blocks, firsts))  8.13 us
    rem x13, other arithmetic, clip_of(): bucket = places // span  8.01 us
    add x9, other arithmetic, update(): total_new = total_old * factor + jnp.sum(weight, axis=-1)  6.27 us
    dot_general x9, matrix products, update(): jnp.einsum('hqk,khd->qhd', weight.astype(jnp.bfloat16), values, preferred...  5.93 us
    transpose x8, other arithmetic, update(): summed_new = summed_old * jnp.transpose(factor)[:, :, None] + added  5.53 us
  transfers between devices with their start and end apart: 8, of which 4 were waited for; matrix products, arithmetic and copies ran while one was open for 15% of the time, Pallas kernels for 0%

commit v1 on v0

v1 whole, which is shorter than its diff:
```python
import jax
import jax.numpy as jnp
from jax import lax
from jax.experimental import pallas as pl
from jax.experimental.pallas import tpu as pltpu
from jax.sharding import Mesh, PartitionSpec as P

HD = 128
HEADS = 3
ROWS = 256
SPAN = 4096
WIDTH = HEADS * HD
SENT = WIDTH + HD
SCALE2 = 1.4426950408889634 / HD**0.5
NEG = -1e30
LOW = -1e20


def clip_at(place, ends):
    return sum((place >= e).astype(jnp.int32) for e in ends)


def attend_kernel(place_ref, lengths_ref, q_own, q_other, *refs):
    kv_refs = refs[:7]
    far_key, far_value, out_ref, score_ref = refs[7:]
    bucket, z, y = place_ref[0], place_ref[1], place_ref[2]
    ends = []
    running = jnp.int32(0)
    for slot in range(3):
        running = running + lengths_ref[bucket, slot]
        ends.append(running)
    key_parts = [(r, 0) for r in kv_refs] + [(far_key, 0)]
    value_parts = [(r, ROWS) for r in kv_refs] + [(far_value, 0)]
    shifts = (0, -1, 1, -2, 2, -3, 3, 4)
    key_starts = [z * (SPAN // 2) + ((y + s) & 7) * ROWS for s in shifts]
    q_starts = [z * (SPAN // 2) + y * ROWS, (1 - z) * (SPAN // 2) + y * ROWS]
    first = clip_at(z * (SPAN // 2), ends)
    same = first == clip_at(z * (SPAN // 2) + SPAN // 2 - 1, ends)
    for q0 in q_starts:
        same &= first == clip_at(q0, ends)
        same &= first == clip_at(q0 + ROWS - 1, ends)

    def body(masked):
        ones = jnp.ones((ROWS, HD), jnp.bfloat16)
        for turn, (q_ref, q0) in enumerate(zip((q_own, q_other), q_starts)):
            row0 = pl.multiple_of((z if turn == 0 else 1 - z) * ROWS, ROWS)
            logs = []
            if masked:
                q_ids = clip_at(q0 + lax.broadcasted_iota(jnp.int32, (ROWS, 1), 0), ends)
            for h in range(HEADS):
                cols = slice(h * HD, (h + 1) * HD)
                buf = (turn * HEADS + h) % 2
                q = q_ref[:, cols]
                peak = None
                for j, (ref, r0) in enumerate(key_parts):
                    k = ref[r0 : r0 + ROWS, cols]
                    s = lax.dot_general(
                        q, k, (((1,), (1,)), ((), ())), preferred_element_type=jnp.float32
                    )
                    if masked:
                        k_ids = clip_at(
                            key_starts[j] + lax.broadcasted_iota(jnp.int32, (1, ROWS), 1), ends
                        )
                        s = jnp.where(q_ids == k_ids, s, NEG)
                    score_ref[buf, :, j * ROWS : (j + 1) * ROWS] = s
                    both = jnp.maximum(s[:, :HD], s[:, HD:])
                    peak = both if peak is None else jnp.maximum(peak, both)
                top = jnp.max(peak, axis=1, keepdims=True)
                if masked:
                    top = jnp.maximum(top, LOW)
                acc = None
                for j, (ref, r0) in enumerate(value_parts):
                    v = jnp.concatenate([ref[r0 : r0 + ROWS, cols], ones], axis=1)
                    s = score_ref[buf, :, j * ROWS : (j + 1) * ROWS]
                    w = jnp.exp2((s - top) * SCALE2).astype(jnp.bfloat16)
                    part = jnp.dot(w, v, preferred_element_type=jnp.float32)
                    acc = part if acc is None else acc + part
                total = acc[:, HD:]
                if masked:
                    total = jnp.maximum(total, 1e-30)
                out_ref[pl.ds(row0, ROWS), cols] = (acc[:, :HD] / total).astype(jnp.bfloat16)
                logs.append(top * SCALE2 + jnp.log2(total[:, :1]))
            lane = lax.broadcasted_iota(jnp.int32, (ROWS, HD), 1)
            packed = jnp.zeros((ROWS, HD), jnp.float32)
            for h in range(HEADS):
                rest = logs[h]
                for piece in range(3):
                    part = rest.astype(jnp.bfloat16).astype(jnp.float32)
                    packed = jnp.where(lane == h * 3 + piece, part, packed)
                    rest = rest - part
            out_ref[pl.ds(row0, ROWS), WIDTH:] = packed.astype(jnp.bfloat16)

    @pl.when(same)
    def _():
        body(False)

    @pl.when(jnp.logical_not(same))
    def _():
        body(True)


def combine_kernel(in_ref, out_ref):
    for m in range(8):
        stats = [in_ref[p * 8 + m, :, WIDTH:].astype(jnp.float32) for p in range(2)]
        for h in range(HEADS):
            logs = [
                s[:, 3 * h : 3 * h + 1] + s[:, 3 * h + 1 : 3 * h + 2] + s[:, 3 * h + 2 : 3 * h + 3]
                for s in stats
            ]
            top = jnp.maximum(logs[0], logs[1])
            w0 = jnp.exp2(logs[0] - top)
            w1 = jnp.exp2(logs[1] - top)
            inv = 1.0 / (w0 + w1)
            cols = slice(h * HD, (h + 1) * HD)
            a = in_ref[m, :, cols].astype(jnp.float32)
            b = in_ref[8 + m, :, cols].astype(jnp.float32)
            mixed = a * (w0 * inv) + b * (w1 * inv)
            out_ref[:, m * WIDTH + h * HD : m * WIDTH + (h + 1) * HD] = mixed.astype(jnp.bfloat16)


def shards(query, key, value, clip_lengths):
    place = jnp.stack([lax.axis_index("b"), lax.axis_index("z"), lax.axis_index("y")])
    place = place.astype(jnp.int32)
    up = [(i, (i + 1) % 8) for i in range(8)]
    down = [(i, (i - 1) % 8) for i in range(8)]
    kv = jnp.concatenate([key, value], axis=0)
    q_other = lax.ppermute(query, "z", [(0, 1), (1, 0)])
    right = left = kv
    blocks = [kv]
    for _ in range(3):
        right = lax.ppermute(right, "y", up)
        left = lax.ppermute(left, "y", down)
        blocks += [right, left]
    far_key = lax.ppermute(right[:ROWS], "y", up)
    far_value = lax.ppermute(left[ROWS:], "y", down)
    vmem = pl.BlockSpec(memory_space=pltpu.VMEM)
    smem = pl.BlockSpec(memory_space=pltpu.SMEM)
    sent = pl.pallas_call(
        attend_kernel,
        out_shape=jax.ShapeDtypeStruct((2 * ROWS, SENT), jnp.bfloat16),
        in_specs=[smem, smem] + [vmem] * 11,
        out_specs=vmem,
        scratch_shapes=[pltpu.VMEM((2, ROWS, SPAN // 2), jnp.float32)],
        compiler_params=pltpu.CompilerParams(vmem_limit_bytes=40 << 20),
        cost_estimate=pl.CostEstimate(
            flops=2 * 2 * 512 * 2048 * 128 * 3, bytes_accessed=4 << 20, transcendentals=3 << 20
        ),
    )(place, clip_lengths, query, q_other, *blocks, far_key, far_value)
    got = lax.all_to_all(
        sent.reshape(16, 32, SENT), ("z", "x", "c"), split_axis=0, concat_axis=0, tiled=True
    )
    return pl.pallas_call(
        combine_kernel,
        out_shape=jax.ShapeDtypeStruct((32, 8 * WIDTH), jnp.bfloat16),
        in_specs=[vmem],
        out_specs=vmem,
    )(got)


def solution(mesh):
    split = Mesh(mesh.devices.reshape(4, 2, 8, 4, 2), ("b", "z", "y", "x", "c"))
    part = P(("b", "z", "y"), ("x", "c"))
    return jax.shard_map(
        shards,
        mesh=split,
        in_specs=(part, part, part, P()),
        out_specs=P(("b", "z", "y", "x", "c"), None),
        check_vma=False,
    )
```

time: 260 us -> 81.7 us (0.31)
  starting transfers between devices: 104 us -> 37 us
  waiting for transfers between devices: 60.5 us -> 12.4 us
  other arithmetic: 45.1 us -> 0.08 us
  local copies, waits for them, and re-layouts: 22 us -> 2.46 us
  matrix products: 10.1 us -> 0 us
  blocking collectives: 11.3 us -> 21.3 us
  Pallas kernels: 0 us -> 7.75 us
  loops' own time: 4.25 us -> 0 us
    ppermute x8 -> x9, starting transfers between devices: 104 us -> 37 us  [the longest x3 17.2 us: shards(): left = lax.ppermute(left, 'y', down)]
    ppermute x8 -> x9, waiting for transfers between devices: 60.5 us -> 12.4 us  [the longest x3 6.63 us: shards(): left = lax.ppermute(left, 'y', down)]
    dot_general x18 -> x0, matrix products: 10.1 us -> none  [the longest x9 5.93 us: update(): jnp.einsum('hqk,khd->qhd', weight.astype(jnp.bfloat16), values, preferred...]
    all_to_all x1, blocking collectives: 11.3 us -> 21.3 us  [shards(): lax.all_to_all(sent.reshape(16, 32, SENT), ('z', 'x', 'c'), split_axis=0,...]
    dynamic_slice x12 -> x0, local copies, waits for them, and re-layouts: 8.13 us -> none  [shards(): lax.scan(step, sweep_carry, (key_blocks, value_blocks, firsts))]
    rem x13 -> x0, other arithmetic: 8.01 us -> none  [clip_of(): bucket = places // span]
    add x21 -> x0, other arithmetic: 7.91 us -> none  [the longest x9 6.27 us: update(): total_new = total_old * factor + jnp.sum(weight, axis=-1)]
    pallas_call x0 -> x2, Pallas kernels: none -> 7.75 us  [the longest x1 5.1 us: shards(): pl.pallas_call(attend_kernel, out_shape=jax.ShapeDtypeStruct((2 * ROWS, S...]
  transfers between devices with their start and end apart: 8 -> 9, of which waited for: 4 -> 4; matrix products, arithmetic and copies ran while one was open for 15% -> 2% of each run, Pallas kernels for 0% -> 0%
where the time goes in v1:
time: 81.7 us; the launch traced here: 81.2 us
  starting transfers between devices  37 us (45%)
  blocking collectives  21.3 us (26%)
  waiting for transfers between devices  12.4 us (15%)
  Pallas kernels  7.75 us (9%)
  local copies, waits for them, and re-layouts  2.46 us (3%)
    all_to_all x1, blocking collectives, shards(): lax.all_to_all(sent.reshape(16, 32, SENT), ('z', 'x', 'c'), split_axis=0,...  21.3 us
    ppermute x3, starting transfers between devices, shards(): left = lax.ppermute(left, 'y', down)  17.2 us
    ppermute x1, starting transfers between devices, shards(): q_other = lax.ppermute(query, 'z', [(0, 1), (1, 0)])  7.55 us
    ppermute x3, waiting for transfers between devices, shards(): left = lax.ppermute(left, 'y', down)  6.63 us
    ppermute x3, starting transfers between devices, shards(): right = lax.ppermute(right, 'y', up)  5.76 us
    ppermute x1, waiting for transfers between devices, shards(): far_key = lax.ppermute(right[:ROWS], 'y', up)  5.62 us
    pallas_call x1, Pallas kernels, shards(): pl.pallas_call(attend_kernel, out_shape=jax.ShapeDtypeStruct((2 * ROWS, S...  5.1 us
    ppermute x1, starting transfers between devices, shards(): far_value = lax.ppermute(left[ROWS:], 'y', down)  4.56 us
  transfers between devices with their start and end apart: 9, of which 4 were waited for; matrix products, arithmetic and copies ran while one was open for 2% of the time, Pallas kernels for 0%

profile of v1, /device:TPU:1, one launch (start us, length us, event | category | flops | bytes accessed | tf_op | source)
XLA Modules:
  0.0 81.2 jit_solution(4071859344367995930)
XLA Ops:
  0.0 0.0 copy-start.2
  0.0 1.0 %constant_dynamic-update-slice_fusion.1 = bf16[512,384]{1,0:T(8,128)(2,1)S(1)} fusion(bf16[256,384]{1,0:T(8,128)(2,1)} %param.5), kind=kLoop, calls=%fused_computation.1 | loop fusion | bytes 393216
  1.0 0.0 copy-done.2
  1.0 0.0 copy-start
  1.1 6.1 %collective-permute-start.2 = (bf16[512,384]{1,0:T(8,128)(2,1)S(1)}, bf16[512,384]{1,0:T(8,128)(2,1)S(1)}, u32[]{:S(2)}, u32[]{:S(2)}) collective-permute-start(bf16[512,384]{1,0:T(8,128)(2,1)S(1)} %constant_dynamic-update-slice_fusion.refs_0_), channel_id=1, source_target_pairs={{0,56},{8,0},{16,8},{24,16},{32,24},{40,32},{48,40},{56,48},{1,57}... | collective-permute-start | bytes 1179656 | tf_op jit(solution)/shard_map/ppermute | solution.py:132
  7.1 1.9 %collective-permute-start.1 = (bf16[512,384]{1,0:T(8,128)(2,1)S(1)}, bf16[512,384]{1,0:T(8,128)(2,1)S(1)}, u32[]{:S(2)}, u32[]{:S(2)}) collective-permute-start(bf16[512,384]{1,0:T(8,128)(2,1)S(1)} %constant_dynamic-update-slice_fusion.refs_0_), channel_id=1, source_target_pairs={{0,8},{8,16},{16,24},{24,32},{32,40},{40,48},{48,56},{56,0},{1,9},... | collective-permute-start | bytes 1179656 | tf_op jit(solution)/shard_map/ppermute | solution.py:131
  9.1 3.9 %collective-permute-done.2.refs_2_ = bf16[512,384]{1,0:T(8,128)(2,1)S(1)} collective-permute-done((bf16[512,384]{1,0:T(8,128)(2,1)S(1)}, bf16[512,384]{1,0:T(8,128)(2,1)S(1)}, u32[]{:S(2)}, u32[]{:S(2)}) %collective-permute-start.2) | collective-permute-done | bytes 393248 | tf_op jit(solution)/shard_map/ppermute | solution.py:132
  12.9 5.3 %collective-permute-start.4 = (bf16[512,384]{1,0:T(8,128)(2,1)S(1)}, bf16[512,384]{1,0:T(8,128)(2,1)S(1)}, u32[]{:S(2)}, u32[]{:S(2)}) collective-permute-start(bf16[512,384]{1,0:T(8,128)(2,1)S(1)} %collective-permute-done.2.refs_2_), channel_id=1, source_target_pairs={{0,56},{8,0},{16,8},{24,16},{32,24},{40,32},{48,40},{56,48},{1,57}... | collective-permute-start | bytes 1179656 | tf_op jit(solution)/shard_map/ppermute | solution.py:132
  18.2 0.0 collective-permute-done.1.refs_1_
  18.2 1.9 %collective-permute-start.3 = (bf16[512,384]{1,0:T(8,128)(2,1)S(1)}, bf16[512,384]{1,0:T(8,128)(2,1)S(1)}, u32[]{:S(2)}, u32[]{:S(2)}) collective-permute-start(bf16[512,384]{1,0:T(8,128)(2,1)S(1)} %collective-permute-done.1.refs_1_), channel_id=1, source_target_pairs={{0,8},{8,16},{16,24},{24,32},{32,40},{40,48},{48,56},{56,0},{1,9},... | collective-permute-start | bytes 1179656 | tf_op jit(solution)/shard_map/ppermute | solution.py:131
  20.2 2.8 %collective-permute-done.4.refs_4_ = bf16[512,384]{1,0:T(8,128)(2,1)S(1)} collective-permute-done((bf16[512,384]{1,0:T(8,128)(2,1)S(1)}, bf16[512,384]{1,0:T(8,128)(2,1)S(1)}, u32[]{:S(2)}, u32[]{:S(2)}) %collective-permute-start.4) | collective-permute-done | bytes 393248 | tf_op jit(solution)/shard_map/ppermute | solution.py:132
  22.9 5.9 %collective-permute-start.6 = (bf16[512,384]{1,0:T(8,128)(2,1)S(1)}, bf16[512,384]{1,0:T(8,128)(2,1)S(1)}, u32[]{:S(2)}, u32[]{:S(2)}) collective-permute-start(bf16[512,384]{1,0:T(8,128)(2,1)S(1)} %collective-permute-done.4.refs_4_), channel_id=1, source_target_pairs={{0,56},{8,0},{16,8},{24,16},{32,24},{40,32},{48,40},{56,48},{1,57}... | collective-permute-start | bytes 1179656 | tf_op jit(solution)/shard_map/ppermute | solution.py:132
  28.8 0.0 collective-permute-done.3.refs_3_
  28.8 1.9 %collective-permute-start.5 = (bf16[512,384]{1,0:T(8,128)(2,1)S(1)}, bf16[512,384]{1,0:T(8,128)(2,1)S(1)}, u32[]{:S(2)}, u32[]{:S(2)}) collective-permute-start(bf16[512,384]{1,0:T(8,128)(2,1)S(1)} %collective-permute-done.3.refs_3_), channel_id=1, source_target_pairs={{0,8},{8,16},{16,24},{24,32},{32,40},{40,48},{48,56},{56,0},{1,9},... | collective-permute-start | bytes 1179656 | tf_op jit(solution)/shard_map/ppermute | solution.py:131
  30.7 0.0 copy-done
  30.8 7.6 %collective-permute-start = (bf16[256,384]{1,0:T(8,128)(2,1)S(1)}, bf16[256,384]{1,0:T(8,128)(2,1)S(1)}, u32[]{:S(2)}, u32[]{:S(2)}) collective-permute-start(bf16[256,384]{1,0:T(8,128)(2,1)S(1)} %copy-done), channel_id=1, source_target_pairs={{0,64},{64,0},{1,65},{65,1},{2,66},{66,2},{3,67},{67,3},{4,68},{68... | collective-permute-start | bytes 589832 | tf_op jit(solution)/shard_map/ppermute | solution.py:127
  38.3 0.0 collective-permute-done.6.refs_6_
  38.3 0.7 slice.9
  39.0 4.6 %collective-permute-start.8 = (bf16[256,384]{1,0:T(8,128)(2,1)}, bf16[256,384]{1,0:T(8,128)(2,1)S(1)}, u32[]{:S(2)}, u32[]{:S(2)}) collective-permute-start(bf16[256,384]{1,0:T(8,128)(2,1)} %slice.9), channel_id=1, source_target_pairs={{0,56},{8,0},{16,8},{24,16},{32,24},{40,32},{48,40},{56,48},{1,57}... | collective-permute-start | bytes 589832 | tf_op jit(solution)/shard_map/ppermute | solution.py:135
  43.6 0.0 collective-permute-done.5.refs_5_
  43.6 0.7 slice.8
  44.3 1.9 %collective-permute-start.7 = (bf16[256,384]{1,0:T(8,128)(2,1)}, bf16[256,384]{1,0:T(8,128)(2,1)S(1)}, u32[]{:S(2)}, u32[]{:S(2)}) collective-permute-start(bf16[256,384]{1,0:T(8,128)(2,1)} %slice.8), channel_id=1, source_target_pairs={{0,8},{8,16},{16,24},{24,32},{32,40},{40,48},{48,56},{56,0},{1,9},... | collective-permute-start | bytes 589832 | tf_op jit(solution)/shard_map/ppermute | solution.py:134
  46.2 0.0 copy-start.1
  46.2 0.1 pad_add_fusion.place_ref
  46.3 0.0 collective-permute-done.q_other
  46.3 0.2 collective-permute-done.8.refs_8_
  46.5 5.6 %collective-permute-done.7.refs_7_ = bf16[256,384]{1,0:T(8,128)(2,1)S(1)} collective-permute-done((bf16[256,384]{1,0:T(8,128)(2,1)}, bf16[256,384]{1,0:T(8,128)(2,1)S(1)}, u32[]{:S(2)}, u32[]{:S(2)}) %collective-permute-start.7) | collective-permute-done | bytes 196640 | tf_op jit(solution)/shard_map/ppermute | solution.py:134
  52.1 0.0 copy-done.1
  52.1 5.1 %shard_map.46 = bf16[512,512]{1,0:T(8,128)(2,1)S(1)} custom-call(s32[3]{0:T(128)S(1)} %pad_add_fusion.place_ref, s32[4,4]{1,0:T(4,128)S(1)} %copy-done.1, bf16[256,384]{1,0:T(8,128)(2,1)S(1)} %copy-done, bf16[256,384]{1,0:T(8,128)(2,1)S(1)} %collective-permute-done.q_other, bf16[512,384]{1,0:T(8,128)(2,1)S(1)} %constant_dynamic-update-slice_fusion.refs_0_, ...), custom_call_target="tpu_custom_call" | custom-call | flops 1610612736 | bytes 4194304 | tf_op jit(solution)/shard_map/pallas_call | solution.py:138
  57.2 21.3 %all_to_all.5.in_ref = bf16[16,32,512]{2,1,0:T(8,128)(2,1)} all-to-all(bf16[16,32,512]{2,1,0:T(8,128)(2,1)S(1)} %bitcast.4), channel_id=1, replica_groups=mesh['b'=4,'z'=2,'y'=8,'x'=4,'c'=2] {'z','x','c'}, dimensions={0} | all-to-all | bytes 1048576 | tf_op jit(solution)/shard_map/all_to_all | solution.py:149
  78.6 2.7 %shard_map.47 = bf16[32,3072]{1,0:T(8,128)(2,1)} custom-call(bf16[16,32,512]{2,1,0:T(8,128)(2,1)} %all_to_all.5.in_ref), custom_call_target="tpu_custom_call" | custom-call | tf_op jit(solution)/shard_map/pallas_call | solution.py:152
  (1 shorter events, 0.0 us)
Async XLA Ops:
  0.0 1.0 %copy-start.2 = (bf16[256,384]{1,0:T(8,128)(2,1)S(1)}, bf16[256,384]{1,0:T(8,128)(2,1)}, u32[]{:S(2)}) copy-start(bf16[256,384]{1,0:T(8,128)(2,1)} %param.6) | copy-start | bytes 589828
  1.0 29.7 %copy-start = (bf16[256,384]{1,0:T(8,128)(2,1)S(1)}, bf16[256,384]{1,0:T(8,128)(2,1)}, u32[]{:S(2)}) copy-start(bf16[256,384]{1,0:T(8,128)(2,1)} %q_own.1) | copy-start | bytes 589828
  1.1 11.9 %collective-permute-start.2 = (bf16[512,384]{1,0:T(8,128)(2,1)S(1)}, bf16[512,384]{1,0:T(8,128)(2,1)S(1)}, u32[]{:S(2)}, u32[]{:S(2)}) collective-permute-start(bf16[512,384]{1,0:T(8,128)(2,1)S(1)} %constant_dynamic-update-slice_fusion.refs_0_), channel_id=1, source_target_pairs={{0,56},{8,0},{16,8},{24,16},{32,24},{40,32},{48,40},{56,48},{1,57}... | collective-permute-start | bytes 1179656 | tf_op jit(solution)/shard_map/ppermute | solution.py:132
  7.1 11.1 %collective-permute-start.1 = (bf16[512,384]{1,0:T(8,128)(2,1)S(1)}, bf16[512,384]{1,0:T(8,128)(2,1)S(1)}, u32[]{:S(2)}, u32[]{:S(2)}) collective-permute-start(bf16[512,384]{1,0:T(8,128)(2,1)S(1)} %constant_dynamic-update-slice_fusion.refs_0_), channel_id=1, source_target_pairs={{0,8},{8,16},{16,24},{24,32},{32,40},{40,48},{48,56},{56,0},{1,9},... | collective-permute-start | bytes 1179656 | tf_op jit(solution)/shard_map/ppermute | solution.py:131
  12.9 10.0 %collective-permute-start.4 = (bf16[512,384]{1,0:T(8,128)(2,1)S(1)}, bf16[512,384]{1,0:T(8,128)(2,1)S(1)}, u32[]{:S(2)}, u32[]{:S(2)}) collective-permute-start(bf16[512,384]{1,0:T(8,128)(2,1)S(1)} %collective-permute-done.2.refs_2_), channel_id=1, source_target_pairs={{0,56},{8,0},{16,8},{24,16},{32,24},{40,32},{48,40},{56,48},{1,57}... | collective-permute-start | bytes 1179656 | tf_op jit(solution)/shard_map/ppermute | solution.py:132
  18.2 10.6 %collective-permute-start.3 = (bf16[512,384]{1,0:T(8,128)(2,1)S(1)}, bf16[512,384]{1,0:T(8,128)(2,1)S(1)}, u32[]{:S(2)}, u32[]{:S(2)}) collective-permute-start(bf16[512,384]{1,0:T(8,128)(2,1)S(1)} %collective-permute-done.1.refs_1_), channel_id=1, source_target_pairs={{0,8},{8,16},{16,24},{24,32},{32,40},{40,48},{48,56},{56,0},{1,9},... | collective-permute-start | bytes 1179656 | tf_op jit(solution)/shard_map/ppermute | solution.py:131
  22.9 15.4 %collective-permute-start.6 = (bf16[512,384]{1,0:T(8,128)(2,1)S(1)}, bf16[512,384]{1,0:T(8,128)(2,1)S(1)}, u32[]{:S(2)}, u32[]{:S(2)}) collective-permute-start(bf16[512,384]{1,0:T(8,128)(2,1)S(1)} %collective-permute-done.4.refs_4_), channel_id=1, source_target_pairs={{0,56},{8,0},{16,8},{24,16},{32,24},{40,32},{48,40},{56,48},{1,57}... | collective-permute-start | bytes 1179656 | tf_op jit(solution)/shard_map/ppermute | solution.py:132
  28.8 14.8 %collective-permute-start.5 = (bf16[512,384]{1,0:T(8,128)(2,1)S(1)}, bf16[512,384]{1,0:T(8,128)(2,1)S(1)}, u32[]{:S(2)}, u32[]{:S(2)}) collective-permute-start(bf16[512,384]{1,0:T(8,128)(2,1)S(1)} %collective-permute-done.3.refs_3_), channel_id=1, source_target_pairs={{0,8},{8,16},{16,24},{24,32},{32,40},{40,48},{48,56},{56,0},{1,9},... | collective-permute-start | bytes 1179656 | tf_op jit(solution)/shard_map/ppermute | solution.py:131
  30.8 15.6 %collective-permute-start = (bf16[256,384]{1,0:T(8,128)(2,1)S(1)}, bf16[256,384]{1,0:T(8,128)(2,1)S(1)}, u32[]{:S(2)}, u32[]{:S(2)}) collective-permute-start(bf16[256,384]{1,0:T(8,128)(2,1)S(1)} %copy-done), channel_id=1, source_target_pairs={{0,64},{64,0},{1,65},{65,1},{2,66},{66,2},{3,67},{67,3},{4,68},{68... | collective-permute-start | bytes 589832 | tf_op jit(solution)/shard_map/ppermute | solution.py:127
  39.0 7.5 %collective-permute-start.8 = (bf16[256,384]{1,0:T(8,128)(2,1)}, bf16[256,384]{1,0:T(8,128)(2,1)S(1)}, u32[]{:S(2)}, u32[]{:S(2)}) collective-permute-start(bf16[256,384]{1,0:T(8,128)(2,1)} %slice.9), channel_id=1, source_target_pairs={{0,56},{8,0},{16,8},{24,16},{32,24},{40,32},{48,40},{56,48},{1,57}... | collective-permute-start | bytes 589832 | tf_op jit(solution)/shard_map/ppermute | solution.py:135
  44.3 7.8 %collective-permute-start.7 = (bf16[256,384]{1,0:T(8,128)(2,1)}, bf16[256,384]{1,0:T(8,128)(2,1)S(1)}, u32[]{:S(2)}, u32[]{:S(2)}) collective-permute-start(bf16[256,384]{1,0:T(8,128)(2,1)} %slice.8), channel_id=1, source_target_pairs={{0,8},{8,16},{16,24},{24,32},{32,40},{40,48},{48,56},{56,0},{1,9},... | collective-permute-start | bytes 589832 | tf_op jit(solution)/shard_map/ppermute | solution.py:134
  46.2 5.9 %copy-start.1 = (s32[4,4]{1,0:T(4,128)S(1)}, s32[4,4]{1,0:T(4,128)}, u32[]{:S(2)}) copy-start(s32[4,4]{1,0:T(4,128)} %lengths_ref.1) | copy-start | bytes 196

commit v2 on v1

v2 whole, which is shorter than its diff:
```python
import jax
import jax.numpy as jnp
from jax import lax
from jax.experimental import pallas as pl
from jax.experimental.pallas import tpu as pltpu
from jax.sharding import Mesh, PartitionSpec as P

HD = 128
HEADS = 3
ROWS = 256
SPAN = 4096
PARTS = 8
WIDTH = HEADS * HD
SENT = WIDTH + HD
SCALE2 = 1.4426950408889634 / HD**0.5
NEG = -1e30
ROOT_SCALE = 16384.0
LOW = -1e20


def clip_at(place, ends):
    return sum((place >= e).astype(jnp.int32) for e in ends)


def attend_kernel(place_ref, lengths_ref, q_own, q_other, kv_ref, out_ref, score_ref):
    bucket, z, y = place_ref[0], place_ref[1], place_ref[2]
    ends = []
    running = jnp.int32(0)
    for slot in range(3):
        running = running + lengths_ref[bucket, slot]
        ends.append(running)
    half = SPAN // 2
    key_start = z * half
    q_starts = [z * half + y * ROWS, (1 - z) * half + y * ROWS]
    first = clip_at(key_start, ends)
    same = first == clip_at(key_start + half - 1, ends)
    for q0 in q_starts:
        same &= first == clip_at(q0, ends)
        same &= first == clip_at(q0 + ROWS - 1, ends)

    def body(masked):
        ones = jnp.ones((ROWS, HD), jnp.bfloat16)
        for turn, (q_ref, q0) in enumerate(zip((q_own, q_other), q_starts)):
            row0 = pl.multiple_of((z if turn == 0 else 1 - z) * ROWS, ROWS)
            logs = []
            if masked:
                q_ids = clip_at(q0 + lax.broadcasted_iota(jnp.int32, (ROWS, 1), 0), ends)
            for h in range(HEADS):
                cols = slice(h * HD, (h + 1) * HD)
                buf = (turn * HEADS + h) % 2
                q = q_ref[:, cols]
                peak = None
                for j in range(PARTS):
                    k = kv_ref[j, 0, :, cols]
                    s = lax.dot_general(
                        q, k, (((1,), (1,)), ((), ())), preferred_element_type=jnp.float32
                    )
                    if masked:
                        k_ids = clip_at(
                            key_start + j * ROWS + lax.broadcasted_iota(jnp.int32, (1, ROWS), 1),
                            ends,
                        )
                        s = jnp.where(q_ids == k_ids, s, NEG)
                    score_ref[buf, :, j * ROWS : (j + 1) * ROWS] = s
                    both = jnp.maximum(s[:, :HD], s[:, HD:])
                    peak = both if peak is None else jnp.maximum(peak, both)
                top = jnp.max(peak, axis=1, keepdims=True)
                if masked:
                    top = jnp.maximum(top, LOW)
                acc = None
                for j in range(PARTS):
                    v = jnp.concatenate([kv_ref[j, 1, :, cols], ones], axis=1)
                    s = score_ref[buf, :, j * ROWS : (j + 1) * ROWS]
                    w = jnp.exp2((s - top) * SCALE2).astype(jnp.bfloat16)
                    part = jnp.dot(w, v, preferred_element_type=jnp.float32)
                    acc = part if acc is None else acc + part
                total = acc[:, HD:]
                if masked:
                    total = jnp.maximum(total, 1e-30)
                out_ref[pl.ds(row0, ROWS), cols] = (acc[:, :HD] / total).astype(jnp.bfloat16)
                logs.append(top * SCALE2 + jnp.log2(total[:, :1]))
            lane = lax.broadcasted_iota(jnp.int32, (ROWS, HD), 1)
            packed = jnp.zeros((ROWS, HD), jnp.float32)
            for h in range(HEADS):
                rest = logs[h]
                for piece in range(3):
                    part = rest.astype(jnp.bfloat16).astype(jnp.float32)
                    packed = jnp.where(lane == h * 3 + piece, part, packed)
                    rest = rest - part
            out_ref[pl.ds(row0, ROWS), WIDTH:] = packed.astype(jnp.bfloat16)

    @pl.when(same)
    def _():
        body(False)

    @pl.when(jnp.logical_not(same))
    def _():
        body(True)


def combine_kernel(in_ref, out_ref):
    lane = lax.broadcasted_iota(jnp.int32, (HD, WIDTH), 0)
    col = lax.broadcasted_iota(jnp.int32, (HD, WIDTH), 1)
    pick = jnp.zeros((HD, WIDTH), jnp.bool_)
    for h in range(HEADS):
        mine = (lane >= 3 * h) & (lane < 3 * h + 3) & (col >= h * HD) & (col < (h + 1) * HD)
        pick = pick | mine
    pick = jnp.where(pick, 1.0, 0.0).astype(jnp.bfloat16)
    for m in range(8):
        log0 = jnp.dot(in_ref[m, :, WIDTH:], pick, preferred_element_type=jnp.float32)
        log1 = jnp.dot(in_ref[8 + m, :, WIDTH:], pick, preferred_element_type=jnp.float32)
        share = 1.0 / (1.0 + jnp.exp2(log0 - log1))
        a = in_ref[m, :, :WIDTH].astype(jnp.float32)
        b = in_ref[8 + m, :, :WIDTH].astype(jnp.float32)
        out_ref[:, m * WIDTH : (m + 1) * WIDTH] = (a + (b - a) * share).astype(jnp.bfloat16)


def shards(query, key, value, clip_lengths):
    place = jnp.stack([lax.axis_index("b"), lax.axis_index("z"), lax.axis_index("y")])
    place = place.astype(jnp.int32)
    q_other = lax.ppermute(query, "z", [(0, 1), (1, 0)])
    kv = jnp.concatenate([key, value], axis=0).astype(jnp.float32)
    sent_kv = (jnp.sign(kv) * jnp.sqrt(jnp.abs(kv)) * ROOT_SCALE).astype(jnp.float16)
    got_kv = lax.all_gather(sent_kv, "y", axis=0, tiled=True).astype(jnp.float32)
    kv_all = (got_kv * jnp.abs(got_kv) * (1.0 / ROOT_SCALE**2)).astype(jnp.bfloat16)
    vmem = pl.BlockSpec(memory_space=pltpu.VMEM)
    smem = pl.BlockSpec(memory_space=pltpu.SMEM)
    sent = pl.pallas_call(
        attend_kernel,
        out_shape=jax.ShapeDtypeStruct((2 * ROWS, SENT), jnp.bfloat16),
        in_specs=[smem, smem] + [vmem] * 3,
        out_specs=vmem,
        scratch_shapes=[pltpu.VMEM((2, ROWS, SPAN // 2), jnp.float32)],
        compiler_params=pltpu.CompilerParams(vmem_limit_bytes=40 << 20),
        cost_estimate=pl.CostEstimate(
            flops=2 * 2 * 512 * 2048 * 128 * 3, bytes_accessed=4 << 20, transcendentals=3 << 20
        ),
    )(place, clip_lengths, query, q_other, kv_all.reshape(PARTS, 2, ROWS, WIDTH))
    got = lax.all_to_all(
        sent.reshape(16, 32, SENT), ("z", "x", "c"), split_axis=0, concat_axis=0, tiled=True
    )
    return pl.pallas_call(
        combine_kernel,
        out_shape=jax.ShapeDtypeStruct((32, 8 * WIDTH), jnp.bfloat16),
        in_specs=[vmem],
        out_specs=vmem,
    )(got)


def solution(mesh):
    split = Mesh(mesh.devices.reshape(4, 2, 8, 4, 2), ("b", "z", "y", "x", "c"))
    part = P(("b", "z", "y"), ("x", "c"))
    return jax.shard_map(
        shards,
        mesh=split,
        in_specs=(part, part, part, P()),
        out_specs=P(("b", "z", "y", "x", "c"), None),
        check_vma=False,
    )
```

time: 81.7 us -> 66 us (0.81)
  starting transfers between devices: 37 us -> 4.82 us
  blocking collectives: 21.3 us -> 51.5 us
  waiting for transfers between devices: 12.4 us -> 0.01 us
  other arithmetic: 0.08 us -> 2.58 us
  local copies, waits for them, and re-layouts: 2.46 us -> 0.01 us
  Pallas kernels: 7.75 us -> 6.9 us
    all_gather x0 -> x1, blocking collectives: none -> 34.5 us  [shards(): lax.all_gather(sent_kv, 'y', axis=0, tiled=True).astype(jnp.float32)]
    ppermute x8 -> x0, starting transfers between devices: 29.5 us -> none  [the longest x3 17.2 us: shards(): left = lax.ppermute(left, 'y', down)]
    ppermute x8 -> x0, waiting for transfers between devices: 12.4 us -> none  [the longest x3 6.63 us: shards(): left = lax.ppermute(left, 'y', down)]
    all_to_all x1, blocking collectives: 21.3 us -> 17 us  [shards(): lax.all_to_all(sent.reshape(16, 32, SENT), ('z', 'x', 'c'), split_axis=0,...]
    ppermute x1, starting transfers between devices: 7.55 us -> 4.82 us  [shards(): q_other = lax.ppermute(query, 'z', [(0, 1), (1, 0)])]
    convert_element_type x0 -> x2, other arithmetic: none -> 2.5 us  [the longest x1 1.53 us: shards(): (jnp.sign(kv) * jnp.sqrt(jnp.abs(kv)) * ROOT_SCALE).astype(jnp.float16)]
    slice x2 -> x0, local copies, waits for them, and re-layouts: 1.4 us -> none  [the longest x1 0.7 us: shards(): far_value = lax.ppermute(left[ROWS:], 'y', down)]
    unnamed x7 -> x4, local copies, waits for them, and re-layouts: 1.03 us -> 0.01 us
  transfers between devices with their start and end apart: 9 -> 1, of which waited for: 4 -> 0; matrix products, arithmetic and copies ran while one was open for 2% -> 4% of each run, Pallas kernels for 0% -> 0%
where the time goes in v2:
time: 66 us; the launch traced here: 65.8 us
  blocking collectives  51.5 us (78%)
  Pallas kernels  6.9 us (10%)
  starting transfers between devices  4.82 us (7%)
  other arithmetic  2.58 us (4%)
    all_gather x1, blocking collectives, shards(): lax.all_gather(sent_kv, 'y', axis=0, tiled=True).astype(jnp.float32)  34.5 us
    all_to_all x1, blocking collectives, shards(): lax.all_to_all(sent.reshape(16, 32, SENT), ('z', 'x', 'c'), split_axis=0,...  17 us
    pallas_call x1, Pallas kernels, shards(): pl.pallas_call(attend_kernel, out_shape=jax.ShapeDtypeStruct((2 * ROWS, S...  4.93 us
    ppermute x1, starting transfers between devices, shards(): q_other = lax.ppermute(query, 'z', [(0, 1), (1, 0)])  4.82 us
    pallas_call x1, Pallas kernels, shards(): pl.pallas_call(combine_kernel, out_shape=jax.ShapeDtypeStruct((32, 8 * WI...  1.98 us
    convert_element_type x1, other arithmetic, shards(): (jnp.sign(kv) * jnp.sqrt(jnp.abs(kv)) * ROOT_SCALE).astype(jnp.float16)  1.53 us
  transfers between devices with their start and end apart: 1, of which 0 were waited for; matrix products, arithmetic and copies ran while one was open for 4% of the time, Pallas kernels for 0%

profile of v2, /device:TPU:1, one launch (start us, length us, event | category | flops | bytes accessed | tf_op | source)
XLA Modules:
  0.0 65.8 jit_solution(14484128307285183360)
XLA Ops:
  0.0 4.8 %collective-permute-start = (bf16[256,384]{1,0:T(8,128)(2,1)}, bf16[256,384]{1,0:T(8,128)(2,1)S(1)}, u32[]{:S(2)}, u32[]{:S(2)}) collective-permute-start(bf16[256,384]{1,0:T(8,128)(2,1)} %q_own.1), channel_id=1, source_target_pairs={{0,64},{64,0},{1,65},{65,1},{2,66},{66,2},{3,67},{67,3},{4,68},{68... | collective-permute-start | bytes 589832 | tf_op jit(solution)/shard_map/ppermute | solution.py:121
  4.8 1.5 %fusion.4 = f16[512,384]{1,0:T(8,128)(2,1)S(1)} fusion(bf16[256,384]{1,0:T(8,128)(2,1)} %param.6, bf16[256,384]{1,0:T(8,128)(2,1)} %param.5), kind=kLoop, calls=%fused_computation.7 | loop fusion | flops 1769472 | bytes 786432 | tf_op jit(solution)/shard_map/convert_element_type | solution.py:123
  6.4 34.5 %all-gather.1 = f16[4096,384]{1,0:T(8,128)(2,1)S(1)} all-gather(f16[512,384]{1,0:T(8,128)(2,1)S(1)} %fusion.4), channel_id=1, replica_groups=mesh['b'=4,'z'=2,'y'=8,'x'=4,'c'=2] {'y'}, dimensions={0}, use_global_device_ids=true | all-gather | bytes 3538944 | tf_op jit(solution)/shard_map/all_gather | solution.py:124
  40.9 0.0 copy-start
  40.9 0.0 copy-start.1
  40.9 1.0 %fusion.1 = bf16[4096,384]{1,0:T(8,128)(2,1)S(1)} fusion(f16[4096,384]{1,0:T(8,128)(2,1)S(1)} %all-gather.1), kind=kLoop, calls=%fused_computation.2 | loop fusion | flops 7864320 | bytes 6291456 | tf_op jit(solution)/shard_map/convert_element_type | solution.py:125
  41.9 0.1 pad_add_fusion.place_ref
  41.9 0.0 collective-permute-done.q_other
  41.9 0.0 copy-done
  41.9 0.0 copy-done.1
  41.9 4.9 %shard_map.46 = bf16[512,512]{1,0:T(8,128)(2,1)S(1)} custom-call(s32[3]{0:T(128)S(1)} %pad_add_fusion.place_ref, s32[4,4]{1,0:T(4,128)S(1)} %copy-done.1, bf16[256,384]{1,0:T(8,128)(2,1)S(1)} %copy-done, bf16[256,384]{1,0:T(8,128)(2,1)S(1)} %collective-permute-done.q_other, bf16[8,2,256,384]{3,2,1,0:T(8,128)(2,1)S(1)} %bitcast.5), custom_call_target="tpu_custom_call" | custom-call | flops 1610612736 | bytes 4194304 | tf_op jit(solution)/shard_map/pallas_call | solution.py:128
  46.9 17.0 %all_to_all.5.in_ref = bf16[16,32,512]{2,1,0:T(8,128)(2,1)} all-to-all(bf16[16,32,512]{2,1,0:T(8,128)(2,1)S(1)} %bitcast.6), channel_id=1, replica_groups=mesh['b'=4,'z'=2,'y'=8,'x'=4,'c'=2] {'z','x','c'}, dimensions={0} | all-to-all | bytes 1048576 | tf_op jit(solution)/shard_map/all_to_all | solution.py:139
  63.8 2.0 %shard_map.47 = bf16[32,3072]{1,0:T(8,128)(2,1)} custom-call(bf16[16,32,512]{2,1,0:T(8,128)(2,1)} %all_to_all.5.in_ref), custom_call_target="tpu_custom_call" | custom-call | tf_op jit(solution)/shard_map/pallas_call | solution.py:142
Async XLA Ops:
  0.0 41.9 %collective-permute-start = (bf16[256,384]{1,0:T(8,128)(2,1)}, bf16[256,384]{1,0:T(8,128)(2,1)S(1)}, u32[]{:S(2)}, u32[]{:S(2)}) collective-permute-start(bf16[256,384]{1,0:T(8,128)(2,1)} %q_own.1), channel_id=1, source_target_pairs={{0,64},{64,0},{1,65},{65,1},{2,66},{66,2},{3,67},{67,3},{4,68},{68... | collective-permute-start | bytes 589832 | tf_op jit(solution)/shard_map/ppermute | solution.py:121
  40.9 1.1 %copy-start = (bf16[256,384]{1,0:T(8,128)(2,1)S(1)}, bf16[256,384]{1,0:T(8,128)(2,1)}, u32[]{:S(2)}) copy-start(bf16[256,384]{1,0:T(8,128)(2,1)} %q_own.1) | copy-start | bytes 589828
  40.9 1.1 %copy-start.1 = (s32[4,4]{1,0:T(4,128)S(1)}, s32[4,4]{1,0:T(4,128)}, u32[]{:S(2)}) copy-start(s32[4,4]{1,0:T(4,128)} %lengths_ref.1) | copy-start | bytes 196

commit v3 on v2

--- a/solution.py
+++ b/solution.py
@@ -40,54 +40,63 @@
 
     def body(masked):
         ones = jnp.ones((ROWS, HD), jnp.bfloat16)
-        for turn, (q_ref, q0) in enumerate(zip((q_own, q_other), q_starts)):
-            row0 = pl.multiple_of((z if turn == 0 else 1 - z) * ROWS, ROWS)
-            logs = []
-            if masked:
-                q_ids = clip_at(q0 + lax.broadcasted_iota(jnp.int32, (ROWS, 1), 0), ends)
-            for h in range(HEADS):
-                cols = slice(h * HD, (h + 1) * HD)
-                buf = (turn * HEADS + h) % 2
-                q = q_ref[:, cols]
-                peak = None
-                for j in range(PARTS):
-                    k = kv_ref[j, 0, :, cols]
+        tiles = [(turn, h) for turn in range(2) for h in range(HEADS)]
+        q_ids = []
+        if masked:
+            rows = lax.broadcasted_iota(jnp.int32, (ROWS, 1), 0)
+            q_ids = [clip_at(q0 + rows, ends) for q0 in q_starts]
+        tops, logs = [], []
+        for i in range(len(tiles) + 1):
+            peak = acc = None
+            for j in range(PARTS):
+                part = slice(j * ROWS, (j + 1) * ROWS)
+                if i < len(tiles):
+                    turn, h = tiles[i]
+                    cols = slice(h * HD, (h + 1) * HD)
                     s = lax.dot_general(
-                        q, k, (((1,), (1,)), ((), ())), preferred_element_type=jnp.float32
+                        (q_own, q_other)[turn][:, cols],
+                        kv_ref[j, 0, :, cols],
+                        (((1,), (1,)), ((), ())),
+                        preferred_element_type=jnp.float32,
                     )
                     if masked:
-                        k_ids = clip_at(
-                            key_start + j * ROWS + lax.broadcasted_iota(jnp.int32, (1, ROWS), 1),
-                            ends,
-                        )
-                        s = jnp.where(q_ids == k_ids, s, NEG)
-                    score_ref[buf, :, j * ROWS : (j + 1) * ROWS] = s
+                        lanes = lax.broadcasted_iota(jnp.int32, (1, ROWS), 1)
+                        k_ids = clip_at(key_start + j * ROWS + lanes, ends)
+                        s = jnp.where(q_ids[turn] == k_ids, s, NEG)
+                    score_ref[i % 2, :, part] = s
                     both = jnp.maximum(s[:, :HD], s[:, HD:])
                     peak = both if peak is None else jnp.maximum(peak, both)
+                if i > 0:
+                    turn, h = tiles[i - 1]
+                    cols = slice(h * HD, (h + 1) * HD)
+                    v = jnp.concatenate([kv_ref[j, 1, :, cols], ones], axis=1)
+                    s = score_ref[(i - 1) % 2, :, part]
+                    w = jnp.exp2((s - tops[i - 1]) * SCALE2).astype(jnp.bfloat16)
+                    more = jnp.dot(w, v, preferred_element_type=jnp.float32)
+                    acc = more if acc is None else acc + more
+            if i < len(tiles):
                 top = jnp.max(peak, axis=1, keepdims=True)
-                if masked:
-                    top = jnp.maximum(top, LOW)
-                acc = None
-                for j in range(PARTS):
-                    v = jnp.concatenate([kv_ref[j, 1, :, cols], ones], axis=1)
-                    s = score_ref[buf, :, j * ROWS : (j + 1) * ROWS]
-                    w = jnp.exp2((s - top) * SCALE2).astype(jnp.bfloat16)
-                    part = jnp.dot(w, v, preferred_element_type=jnp.float32)
-                    acc = part if acc is None else acc + part
+                tops.append(jnp.maximum(top, LOW) if masked else top)
+            if i > 0:
+                turn, h = tiles[i - 1]
+                row0 = pl.multiple_of((z if turn == 0 else 1 - z) * ROWS, ROWS)
                 total = acc[:, HD:]
                 if masked:
                     total = jnp.maximum(total, 1e-30)
-                out_ref[pl.ds(row0, ROWS), cols] = (acc[:, :HD] / total).astype(jnp.bfloat16)
-                logs.append(top * SCALE2 + jnp.log2(total[:, :1]))
-            lane = lax.broadcasted_iota(jnp.int32, (ROWS, HD), 1)
-            packed = jnp.zeros((ROWS, HD), jnp.float32)
-            for h in range(HEADS):
-                rest = logs[h]
-                for piece in range(3):
-                    part = rest.astype(jnp.bfloat16).astype(jnp.float32)
-                    packed = jnp.where(lane == h * 3 + piece, part, packed)
-                    rest = rest - part
-            out_ref[pl.ds(row0, ROWS), WIDTH:] = packed.astype(jnp.bfloat16)
+                out_ref[pl.ds(row0, ROWS), h * HD : (h + 1) * HD] = (acc[:, :HD] / total).astype(
+                    jnp.bfloat16
+                )
+                logs.append(tops[i - 1] * SCALE2 + jnp.log2(total[:, :1]))
+                if h == HEADS - 1:
+                    lane = lax.broadcasted_iota(jnp.int32, (ROWS, HD), 1)
+                    packed = jnp.zeros((ROWS, HD), jnp.float32)
+                    for hh in range(HEADS):
+                        rest = logs[turn * HEADS + hh]
+                        for piece in range(3):
+                            high = rest.astype(jnp.bfloat16).astype(jnp.float32)
+                            packed = jnp.where(lane == hh * 3 + piece, high, packed)
+                            rest = rest - high
+                    out_ref[pl.ds(row0, ROWS), WIDTH:] = packed.astype(jnp.bfloat16)
 
     @pl.when(same)
     def _():
@@ -144,6 +153,7 @@
         out_shape=jax.ShapeDtypeStruct((32, 8 * WIDTH), jnp.bfloat16),
         in_specs=[vmem],
         out_specs=vmem,
+        compiler_params=pltpu.CompilerParams(vmem_limit_bytes=4 << 20),
     )(got)
 
 

time: 66 us -> 64.5 us (0.977)
  Pallas kernels: 6.9 us -> 5.55 us
    pallas_call x1, Pallas kernels: 1.98 us -> 0.95 us  [shards(): pl.pallas_call(combine_kernel, out_shape=jax.ShapeDtypeStruct((32, 8 * WI...]
where the time goes in v3:
time: 64.5 us; the launch traced here: 64.3 us
  blocking collectives  51.3 us (80%)
  Pallas kernels  5.55 us (9%)
  starting transfers between devices  4.82 us (7%)
  other arithmetic  2.58 us (4%)
    all_gather x1, blocking collectives, shards(): lax.all_gather(sent_kv, 'y', axis=0, tiled=True).astype(jnp.float32)  34.5 us
    all_to_all x1, blocking collectives, shards(): lax.all_to_all(sent.reshape(16, 32, SENT), ('z', 'x', 'c'), split_axis=0,...  16.8 us
    ppermute x1, starting transfers between devices, shards(): q_other = lax.ppermute(query, 'z', [(0, 1), (1, 0)])  4.82 us
    pallas_call x1, Pallas kernels, shards(): pl.pallas_call(attend_kernel, out_shape=jax.ShapeDtypeStruct((2 * ROWS, S...  4.6 us
    convert_element_type x1, other arithmetic, shards(): (jnp.sign(kv) * jnp.sqrt(jnp.abs(kv)) * ROOT_SCALE).astype(jnp.float16)  1.53 us
  transfers between devices with their start and end apart: 1, of which 0 were waited for; matrix products, arithmetic and copies ran while one was open for 4% of the time, Pallas kernels for 0%

profile of v3, /device:TPU:1, one launch (start us, length us, event | category | flops | bytes accessed | tf_op | source)
XLA Modules:
  0.0 64.3 jit_solution(4566218727640878062)
XLA Ops:
  0.0 4.8 %collective-permute-start = (bf16[256,384]{1,0:T(8,128)(2,1)}, bf16[256,384]{1,0:T(8,128)(2,1)S(1)}, u32[]{:S(2)}, u32[]{:S(2)}) collective-permute-start(bf16[256,384]{1,0:T(8,128)(2,1)} %q_own.1), channel_id=1, source_target_pairs={{0,64},{64,0},{1,65},{65,1},{2,66},{66,2},{3,67},{67,3},{4,68},{68... | collective-permute-start | bytes 589832 | tf_op jit(solution)/shard_map/ppermute | solution.py:130
  4.8 1.5 %fusion.4 = f16[512,384]{1,0:T(8,128)(2,1)S(1)} fusion(bf16[256,384]{1,0:T(8,128)(2,1)} %param.6, bf16[256,384]{1,0:T(8,128)(2,1)} %param.5), kind=kLoop, calls=%fused_computation.7 | loop fusion | flops 1769472 | bytes 786432 | tf_op jit(solution)/shard_map/convert_element_type | solution.py:132
  6.4 34.5 %all-gather.1 = f16[4096,384]{1,0:T(8,128)(2,1)S(1)} all-gather(f16[512,384]{1,0:T(8,128)(2,1)S(1)} %fusion.4), channel_id=1, replica_groups=mesh['b'=4,'z'=2,'y'=8,'x'=4,'c'=2] {'y'}, dimensions={0}, use_global_device_ids=true | all-gather | bytes 3538944 | tf_op jit(solution)/shard_map/all_gather | solution.py:133
  40.9 0.0 copy-start
  40.9 0.0 copy-start.1
  40.9 1.0 %fusion.1 = bf16[4096,384]{1,0:T(8,128)(2,1)S(1)} fusion(f16[4096,384]{1,0:T(8,128)(2,1)S(1)} %all-gather.1), kind=kLoop, calls=%fused_computation.2 | loop fusion | flops 7864320 | bytes 6291456 | tf_op jit(solution)/shard_map/convert_element_type | solution.py:134
  41.9 0.1 pad_add_fusion.place_ref
  41.9 0.0 collective-permute-done.q_other
  41.9 0.0 copy-done
  41.9 0.0 copy-done.1
  41.9 4.6 %shard_map.46 = bf16[512,512]{1,0:T(8,128)(2,1)S(1)} custom-call(s32[3]{0:T(128)S(1)} %pad_add_fusion.place_ref, s32[4,4]{1,0:T(4,128)S(1)} %copy-done.1, bf16[256,384]{1,0:T(8,128)(2,1)S(1)} %copy-done, bf16[256,384]{1,0:T(8,128)(2,1)S(1)} %collective-permute-done.q_other, bf16[8,2,256,384]{3,2,1,0:T(8,128)(2,1)S(1)} %bitcast.5), custom_call_target="tpu_custom_call" | custom-call | flops 1610612736 | bytes 4194304 | tf_op jit(solution)/shard_map/pallas_call | solution.py:137
  46.6 16.8 %all_to_all.5.in_ref = bf16[16,32,512]{2,1,0:T(8,128)(2,1)S(1)} all-to-all(bf16[16,32,512]{2,1,0:T(8,128)(2,1)S(1)} %bitcast.6), channel_id=1, replica_groups=mesh['b'=4,'z'=2,'y'=8,'x'=4,'c'=2] {'z','x','c'}, dimensions={0} | all-to-all | bytes 1048576 | tf_op jit(solution)/shard_map/all_to_all | solution.py:148
  63.4 0.9 %shard_map.47 = bf16[32,3072]{1,0:T(8,128)(2,1)} custom-call(bf16[16,32,512]{2,1,0:T(8,128)(2,1)S(1)} %all_to_all.5.in_ref), custom_call_target="tpu_custom_call" | custom-call | tf_op jit(solution)/shard_map/pallas_call | solution.py:151
Async XLA Ops:
  0.0 41.9 %collective-permute-start = (bf16[256,384]{1,0:T(8,128)(2,1)}, bf16[256,384]{1,0:T(8,128)(2,1)S(1)}, u32[]{:S(2)}, u32[]{:S(2)}) collective-permute-start(bf16[256,384]{1,0:T(8,128)(2,1)} %q_own.1), channel_id=1, source_target_pairs={{0,64},{64,0},{1,65},{65,1},{2,66},{66,2},{3,67},{67,3},{4,68},{68... | collective-permute-start | bytes 589832 | tf_op jit(solution)/shard_map/ppermute | solution.py:130
  40.9 1.1 %copy-start = (bf16[256,384]{1,0:T(8,128)(2,1)S(1)}, bf16[256,384]{1,0:T(8,128)(2,1)}, u32[]{:S(2)}) copy-start(bf16[256,384]{1,0:T(8,128)(2,1)} %q_own.1) | copy-start | bytes 589828
  40.9 1.1 %copy-start.1 = (s32[4,4]{1,0:T(4,128)S(1)}, s32[4,4]{1,0:T(4,128)}, u32[]{:S(2)}) copy-start(s32[4,4]{1,0:T(4,128)} %lengths_ref.1) | copy-start | bytes 196

commit v4 on v3

--- a/solution.py
+++ b/solution.py
@@ -11,7 +11,8 @@
 SPAN = 4096
 PARTS = 8
 WIDTH = HEADS * HD
-SENT = WIDTH + HD
+CHUNK = 32
+SENT = WIDTH // HD * CHUNK + 8
 SCALE2 = 1.4426950408889634 / HD**0.5
 NEG = -1e30
 ROOT_SCALE = 16384.0
@@ -79,13 +80,15 @@
                 tops.append(jnp.maximum(top, LOW) if masked else top)
             if i > 0:
                 turn, h = tiles[i - 1]
-                row0 = pl.multiple_of((z if turn == 0 else 1 - z) * ROWS, ROWS)
+                side = z if turn == 0 else 1 - z
                 total = acc[:, HD:]
                 if masked:
                     total = jnp.maximum(total, 1e-30)
-                out_ref[pl.ds(row0, ROWS), h * HD : (h + 1) * HD] = (acc[:, :HD] / total).astype(
-                    jnp.bfloat16
-                )
+                mean = (acc[:, :HD] / total).astype(jnp.bfloat16)
+                for m in range(8):
+                    out_ref[2 * m + side, h * CHUNK : (h + 1) * CHUNK, :] = mean[
+                        m * CHUNK : (m + 1) * CHUNK
+                    ]
                 logs.append(tops[i - 1] * SCALE2 + jnp.log2(total[:, :1]))
                 if h == HEADS - 1:
                     lane = lax.broadcasted_iota(jnp.int32, (ROWS, HD), 1)
@@ -96,7 +99,12 @@
                             high = rest.astype(jnp.bfloat16).astype(jnp.float32)
                             packed = jnp.where(lane == hh * 3 + piece, high, packed)
                             rest = rest - high
-                    out_ref[pl.ds(row0, ROWS), WIDTH:] = packed.astype(jnp.bfloat16)
+                    for m in range(8):
+                        tile = packed[m * CHUNK : m * CHUNK + 8]
+                        for g in range(1, 4):
+                            rows8 = packed[m * CHUNK + 8 * g : m * CHUNK + 8 * g + 8]
+                            tile = tile + pltpu.roll(rows8, 16 * g, 1)
+                        out_ref[2 * m + side, HEADS * CHUNK :, :] = tile.astype(jnp.bfloat16)
 
     @pl.when(same)
     def _():
@@ -108,20 +116,26 @@
 
 
 def combine_kernel(in_ref, out_ref):
+    tiles = in_ref[:, HEADS * CHUNK :, :].astype(jnp.float32).reshape(128, HD)
+    tiles = tiles.astype(jnp.bfloat16)
     lane = lax.broadcasted_iota(jnp.int32, (HD, WIDTH), 0)
-    col = lax.broadcasted_iota(jnp.int32, (HD, WIDTH), 1)
-    pick = jnp.zeros((HD, WIDTH), jnp.bool_)
-    for h in range(HEADS):
-        mine = (lane >= 3 * h) & (lane < 3 * h + 3) & (col >= h * HD) & (col < (h + 1) * HD)
-        pick = pick | mine
-    pick = jnp.where(pick, 1.0, 0.0).astype(jnp.bfloat16)
+    head = lax.broadcasted_iota(jnp.int32, (HD, WIDTH), 1) // HD
+    shares = []
+    for g in range(4):
+        low = 16 * g + 3 * head
+        pick = jnp.where((lane >= low) & (lane < low + 3), 1.0, 0.0).astype(jnp.bfloat16)
+        shares.append(jnp.dot(tiles, pick, preferred_element_type=jnp.float32))
     for m in range(8):
-        log0 = jnp.dot(in_ref[m, :, WIDTH:], pick, preferred_element_type=jnp.float32)
-        log1 = jnp.dot(in_ref[8 + m, :, WIDTH:], pick, preferred_element_type=jnp.float32)
-        share = 1.0 / (1.0 + jnp.exp2(log0 - log1))
-        a = in_ref[m, :, :WIDTH].astype(jnp.float32)
-        b = in_ref[8 + m, :, :WIDTH].astype(jnp.float32)
-        out_ref[:, m * WIDTH : (m + 1) * WIDTH] = (a + (b - a) * share).astype(jnp.bfloat16)
+        logs = [
+            jnp.concatenate([s[8 * (2 * m + p) : 8 * (2 * m + p) + 8] for s in shares], axis=0)
+            for p in range(2)
+        ]
+        share = 1.0 / (1.0 + jnp.exp2(logs[0] - logs[1]))
+        for h in range(HEADS):
+            a = in_ref[2 * m, h * CHUNK : (h + 1) * CHUNK, :].astype(jnp.float32)
+            b = in_ref[2 * m + 1, h * CHUNK : (h + 1) * CHUNK, :].astype(jnp.float32)
+            mixed = a + (b - a) * share[:, h * HD : (h + 1) * HD]
+            out_ref[:, m * WIDTH + h * HD : m * WIDTH + (h + 1) * HD] = mixed.astype(jnp.bfloat16)
 
 
 def shards(query, key, value, clip_lengths):
@@ -129,14 +143,14 @@
     place = place.astype(jnp.int32)
     q_other = lax.ppermute(query, "z", [(0, 1), (1, 0)])
     kv = jnp.concatenate([key, value], axis=0).astype(jnp.float32)
-    sent_kv = (jnp.sign(kv) * jnp.sqrt(jnp.abs(kv)) * ROOT_SCALE).astype(jnp.float16)
+    sent_kv = (kv * lax.rsqrt(jnp.maximum(jnp.abs(kv), 1e-36)) * ROOT_SCALE).astype(jnp.float16)
     got_kv = lax.all_gather(sent_kv, "y", axis=0, tiled=True).astype(jnp.float32)
     kv_all = (got_kv * jnp.abs(got_kv) * (1.0 / ROOT_SCALE**2)).astype(jnp.bfloat16)
     vmem = pl.BlockSpec(memory_space=pltpu.VMEM)
     smem = pl.BlockSpec(memory_space=pltpu.SMEM)
     sent = pl.pallas_call(
         attend_kernel,
-        out_shape=jax.ShapeDtypeStruct((2 * ROWS, SENT), jnp.bfloat16),
+        out_shape=jax.ShapeDtypeStruct((16, SENT, HD), jnp.bfloat16),
         in_specs=[smem, smem] + [vmem] * 3,
         out_specs=vmem,
         scratch_shapes=[pltpu.VMEM((2, ROWS, SPAN // 2), jnp.float32)],
@@ -145,9 +159,7 @@
             flops=2 * 2 * 512 * 2048 * 128 * 3, bytes_accessed=4 << 20, transcendentals=3 << 20
         ),
     )(place, clip_lengths, query, q_other, kv_all.reshape(PARTS, 2, ROWS, WIDTH))
-    got = lax.all_to_all(
-        sent.reshape(16, 32, SENT), ("z", "x", "c"), split_axis=0, concat_axis=0, tiled=True
-    )
+    got = lax.all_to_all(sent, ("x", "c", "z"), split_axis=0, concat_axis=0, tiled=True)
     return pl.pallas_call(
         combine_kernel,
         out_shape=jax.ShapeDtypeStruct((32, 8 * WIDTH), jnp.bfloat16),

time: 64.5 us -> 63.4 us (0.983)
  blocking collectives: 51.3 us -> 50.2 us
    all_to_all x1, blocking collectives: 16.8 us -> 15.7 us  [shards(): lax.all_to_all(sent, ('x', 'c', 'z'), split_axis=0, concat_axis=0, tiled=...]
where the time goes in v4:
time: 63.4 us; the launch traced here: 63.2 us
  blocking collectives  50.2 us (79%)
  Pallas kernels  5.93 us (9%)
  starting transfers between devices  4.82 us (8%)
  other arithmetic  2.28 us (4%)
    all_gather x1, blocking collectives, shards(): lax.all_gather(sent_kv, 'y', axis=0, tiled=True).astype(jnp.float32)  34.5 us
    all_to_all x1, blocking collectives, shards(): lax.all_to_all(sent, ('x', 'c', 'z'), split_axis=0, concat_axis=0, tiled=...  15.7 us
    pallas_call x1, Pallas kernels, shards(): pl.pallas_call(attend_kernel, out_shape=jax.ShapeDtypeStruct((16, SENT, H...  4.95 us
    ppermute x1, starting transfers between devices, shards(): q_other = lax.ppermute(query, 'z', [(0, 1), (1, 0)])  4.82 us
  transfers between devices with their start and end apart: 1, of which 0 were waited for; matrix products, arithmetic and copies ran while one was open for 4% of the time, Pallas kernels for 0%

profile of v4, /device:TPU:1, one launch (start us, length us, event | category | flops | bytes accessed | tf_op | source)
XLA Modules:
  0.0 63.2 jit_solution(5686342277186528558)
XLA Ops:
  0.0 4.8 %collective-permute-start = (bf16[256,384]{1,0:T(8,128)(2,1)}, bf16[256,384]{1,0:T(8,128)(2,1)S(1)}, u32[]{:S(2)}, u32[]{:S(2)}) collective-permute-start(bf16[256,384]{1,0:T(8,128)(2,1)} %q_own.1), channel_id=1, source_target_pairs={{0,64},{64,0},{1,65},{65,1},{2,66},{66,2},{3,67},{67,3},{4,68},{68... | collective-permute-start | bytes 589832 | tf_op jit(solution)/shard_map/ppermute | solution.py:144
  4.8 1.2 %fusion.5 = f16[512,384]{1,0:T(8,128)(2,1)S(1)} fusion(bf16[256,384]{1,0:T(8,128)(2,1)} %param.6, bf16[256,384]{1,0:T(8,128)(2,1)} %param.5), kind=kLoop, calls=%fused_computation.8 | loop fusion | flops 1769472 | bytes 786432 | tf_op jit(solution)/shard_map/convert_element_type | solution.py:146
  6.1 34.5 %all-gather.1 = f16[4096,384]{1,0:T(8,128)(2,1)S(1)} all-gather(f16[512,384]{1,0:T(8,128)(2,1)S(1)} %fusion.5), channel_id=1, replica_groups=mesh['b'=4,'z'=2,'y'=8,'x'=4,'c'=2] {'y'}, dimensions={0}, use_global_device_ids=true | all-gather | bytes 3538944 | tf_op jit(solution)/shard_map/all_gather | solution.py:147
  40.6 0.0 copy-start
  40.6 0.0 copy-start.1
  40.6 1.0 %fusion.1 = bf16[4096,384]{1,0:T(8,128)(2,1)S(1)} fusion(f16[4096,384]{1,0:T(8,128)(2,1)S(1)} %all-gather.1), kind=kLoop, calls=%fused_computation.2 | loop fusion | flops 7864320 | bytes 6291456 | tf_op jit(solution)/shard_map/convert_element_type | solution.py:148
  41.6 0.1 pad_add_fusion.place_ref
  41.6 0.0 collective-permute-done.q_other
  41.6 0.0 copy-done
  41.6 0.0 copy-done.1
  41.6 4.9 %shard_map.46 = bf16[16,104,128]{2,1,0:T(8,128)(2,1)S(1)} custom-call(s32[3]{0:T(128)S(1)} %pad_add_fusion.place_ref, s32[4,4]{1,0:T(4,128)S(1)} %copy-done.1, bf16[256,384]{1,0:T(8,128)(2,1)S(1)} %copy-done, bf16[256,384]{1,0:T(8,128)(2,1)S(1)} %collective-permute-done.q_other, bf16[8,2,256,384]{3,2,1,0:T(8,128)(2,1)S(1)} %bitcast.4), custom_call_target="tpu_custom_call" | custom-call | flops 1610612736 | bytes 4194304 | tf_op jit(solution)/shard_map/pallas_call | solution.py:151
  46.6 15.7 %all_to_all.5.in_ref = bf16[16,104,128]{2,1,0:T(8,128)(2,1)S(1)} all-to-all(bf16[16,104,128]{2,1,0:T(8,128)(2,1)S(1)} %shard_map.46), channel_id=1, replica_groups=mesh['b'=4,'z'=2,'y'=8,'x'=4,'c'=2] {'x','c','z'}, dimensions={0} | all-to-all | bytes 851968 | tf_op jit(solution)/shard_map/all_to_all | solution.py:162
  62.3 1.0 %shard_map.47 = bf16[32,3072]{1,0:T(8,128)(2,1)} custom-call(bf16[16,104,128]{2,1,0:T(8,128)(2,1)S(1)} %all_to_all.5.in_ref), custom_call_target="tpu_custom_call" | custom-call | tf_op jit(solution)/shard_map/pallas_call | solution.py:163
Async XLA Ops:
  0.0 41.6 %collective-permute-start = (bf16[256,384]{1,0:T(8,128)(2,1)}, bf16[256,384]{1,0:T(8,128)(2,1)S(1)}, u32[]{:S(2)}, u32[]{:S(2)}) collective-permute-start(bf16[256,384]{1,0:T(8,128)(2,1)} %q_own.1), channel_id=1, source_target_pairs={{0,64},{64,0},{1,65},{65,1},{2,66},{66,2},{3,67},{67,3},{4,68},{68... | collective-permute-start | bytes 589832 | tf_op jit(solution)/shard_map/ppermute | solution.py:144
  40.6 1.1 %copy-start = (bf16[256,384]{1,0:T(8,128)(2,1)S(1)}, bf16[256,384]{1,0:T(8,128)(2,1)}, u32[]{:S(2)}) copy-start(bf16[256,384]{1,0:T(8,128)(2,1)} %q_own.1) | copy-start | bytes 589828
  40.6 1.1 %copy-start.1 = (s32[4,4]{1,0:T(4,128)S(1)}, s32[4,4]{1,0:T(4,128)}, u32[]{:S(2)}) copy-start(s32[4,4]{1,0:T(4,128)} %lengths_ref.1) | copy-start | bytes 196
